TPU v7x, 256 devices: a whole 4x4x8 slice. The times are simulated.
256 devices in a mesh: ctx: 32 (over z, x), ch: 8 (over y, core).
Axes of the slice: x: 4, y: 4, z: 8, core: 2. Of those that a mesh axis runs over, the one named last changes fastest.
Arguments:
- query_input: bfloat16 [4096, 4096], P('ctx', 'ch'), may hold values from -6 to 6
- key_input: bfloat16 [4096, 4096], P('ctx', 'ch'), may hold values from -6 to 6
- value_input: bfloat16 [4096, 4096], P('ctx', 'ch'), may hold values from -6 to 6
- short_weight: float32 [3, 3, 4096], P(None, None, 'ch'), may hold values from -3.5 to 3.5
- residue: float32 [16, 4096], P(None, 'ch'), may hold values from -1.5 to 1.5
- decay_rate: float32 [16, 4096], P(None, 'ch'), may hold values from 0.00012207031 to 0.05
- skip_gain: float32 [4096], P('ch'), may hold values from -1 to 1
- out_weight: bfloat16 [4096, 8192], P('ch'), may hold values from -0.125 to 0.125
Outputs:
- layer_output: bfloat16 [4096, 8192], P('ctx', 'ch')
All inputs are finite; a program needn't handle non-finite values.
Results may differ from a plain program's by a relative error of at most 0.015.
Values may be sent and summed in bfloat16 or wider, within the bound.
No kernel may reach another device: no remote copies, remote signals or barrier semaphores. Data moves between devices by JAX's collectives and lax.ppermute only.
A program may use at most 64 MiB of HBM per device.

v0:
```python
import math

import jax
import jax.numpy as jnp
import numpy as np
from jax import lax
from jax.sharding import PartitionSpec as P

HIGHEST = lax.Precision.HIGHEST


def swapped(value, axis, apart):
    mask = 2**apart
    pairs = [(source, source ^ mask) for source in range(lax.axis_size(axis))]
    return lax.ppermute(value, axis, pairs)


def passed_along(block, axis, distance):
    devices = range(lax.axis_size(axis))
    route = [(i - distance, i) for i in devices if i - distance in devices]
    return lax.ppermute(block, axis, route)


def short_filter(raw_rows, prior_rows, taps):
    extended = jnp.concatenate([prior_rows, raw_rows], axis=0).astype(jnp.float32)
    length_rows = raw_rows.shape[0]
    tap_count = taps.shape[0]
    running = jnp.zeros(raw_rows.shape, jnp.float32)
    for offset in range(tap_count):
        running = (
            running
            + taps[offset] * extended[tap_count - 1 - offset : tap_count - 1 - offset + length_rows]
        )
    return running


def reversed_index(device_index, bit_total):
    running = jnp.zeros((), jnp.int32)
    for position in range(bit_total):
        running = running + (device_index >> position & 1) * (1 << bit_total - 1 - position)
    return running


def local_matrix(row_count, sign_value):
    products = np.outer(np.arange(row_count), np.arange(row_count)) % row_count
    phases = sign_value * 2.0 * math.pi * products / row_count
    return (jnp.asarray(np.cos(phases), jnp.float32), jnp.asarray(np.sin(phases), jnp.float32))


def across_rows(real_part, imag_part, sign_value):
    mat_real, mat_imag = local_matrix(real_part.shape[1], sign_value)
    out_real = jnp.einsum("kb,ebc->ekc", mat_real, real_part, precision=HIGHEST) - jnp.einsum(
        "kb,ebc->ekc", mat_imag, imag_part, precision=HIGHEST
    )
    out_imag = jnp.einsum("kb,ebc->ekc", mat_real, imag_part, precision=HIGHEST) + jnp.einsum(
        "kb,ebc->ekc", mat_imag, real_part, precision=HIGHEST
    )
    return (out_real, out_imag)


def rotate_rows(real_part, imag_part, frequency_row, sign_value, total_rows):
    products = jnp.arange(real_part.shape[1], dtype=jnp.int32) * frequency_row
    phases = sign_value * 2.0 * math.pi / total_rows * products.astype(jnp.float32)
    cosine = jnp.cos(phases)[None, :, None]
    sine_value = jnp.sin(phases)[None, :, None]
    return (
        real_part * cosine - imag_part * sine_value,
        real_part * sine_value + imag_part * cosine,
    )


def pairs_forward(real_part, imag_part, device_index, bit_total):
    for section_bit in reversed(range(bit_total)):
        other_real, other_imag = swapped((real_part, imag_part), "ctx", section_bit)
        higher = device_index >> section_bit & 1 == 1
        within = (device_index % (1 << section_bit)).astype(jnp.float32)
        phase_angle = -2.0 * math.pi * within / float(2 << section_bit)
        cosine = jnp.cos(phase_angle)
        sine_value = jnp.sin(phase_angle)
        diff_real = other_real - real_part
        diff_imag = other_imag - imag_part
        turned_real = diff_real * cosine - diff_imag * sine_value
        turned_imag = diff_real * sine_value + diff_imag * cosine
        real_part = jnp.where(higher, turned_real, real_part + other_real)
        imag_part = jnp.where(higher, turned_imag, imag_part + other_imag)
    return (real_part, imag_part)


def pairs_inverse(real_part, imag_part, device_index, bit_total):
    for section_bit in range(bit_total):
        higher = device_index >> section_bit & 1 == 1
        within = (device_index % (1 << section_bit)).astype(jnp.float32)
        phase_angle = 2.0 * math.pi * within / float(2 << section_bit)
        cosine = jnp.cos(phase_angle)
        sine_value = jnp.sin(phase_angle)
        ready_real = jnp.where(higher, real_part * cosine - imag_part * sine_value, real_part)
        ready_imag = jnp.where(higher, real_part * sine_value + imag_part * cosine, imag_part)
        other_real, other_imag = swapped((ready_real, ready_imag), "ctx", section_bit)
        real_part = jnp.where(higher, other_real - ready_real, ready_real + other_real)
        imag_part = jnp.where(higher, other_imag - ready_imag, ready_imag + other_imag)
    return (real_part, imag_part)


def forward_spectrum(local_rows, device_index, frequency_row, total_rows):
    row_count = local_rows.shape[0]
    bit_total = lax.axis_size("ctx").bit_length() - 1
    positions = (device_index * row_count + jnp.arange(row_count, dtype=jnp.int32)).astype(
        jnp.float32
    )[:, None]
    phases = -math.pi / total_rows * positions
    real_part = jnp.stack([local_rows, local_rows * jnp.cos(phases)])
    imag_part = jnp.stack([jnp.zeros_like(local_rows), local_rows * jnp.sin(phases)])
    real_part, imag_part = pairs_forward(real_part, imag_part, device_index, bit_total)
    real_part, imag_part = rotate_rows(real_part, imag_part, frequency_row, -1.0, total_rows)
    return across_rows(real_part, imag_part, -1.0)


def inverse_rows(real_part, imag_part, device_index, frequency_row, total_rows):
    row_count = real_part.shape[1]
    bit_total = lax.axis_size("ctx").bit_length() - 1
    real_part, imag_part = across_rows(real_part, imag_part, 1.0)
    real_part, imag_part = rotate_rows(real_part, imag_part, frequency_row, 1.0, total_rows)
    real_part, imag_part = pairs_inverse(real_part, imag_part, device_index, bit_total)
    positions = (device_index * row_count + jnp.arange(row_count, dtype=jnp.int32)).astype(
        jnp.float32
    )[:, None]
    phases = math.pi / total_rows * positions
    combined = real_part[0] + real_part[1] * jnp.cos(phases) - imag_part[1] * jnp.sin(phases)
    return combined / (2.0 * total_rows)


def closed_spectrum(residue, decay_rate, frequencies, total_rows):
    angle = math.pi / total_rows * frequencies.astype(jnp.float32)
    cos_angle = jnp.cos(angle)[:, :, None]
    sin_angle = jnp.sin(angle)[:, :, None]
    versine = (2.0 * jnp.sin(0.5 * angle) ** 2)[:, :, None]
    parity = (1 - 2 * (frequencies % 2)).astype(jnp.float32)[:, :, None]
    shape_out = (frequencies.shape[0], frequencies.shape[1], residue.shape[1])
    spec_real = jnp.zeros(shape_out, jnp.float32)
    spec_imag = jnp.zeros(shape_out, jnp.float32)
    for order_mode in range(residue.shape[0]):
        rate = decay_rate[order_mode]
        amplitude = residue[order_mode] * jnp.sqrt(2.0 * rate)
        lost = -jnp.expm1(-rate)
        retained = jnp.exp(-rate)
        tail = jnp.exp(-rate * total_rows)
        numerator = amplitude * (1.0 - tail * parity)
        den_real = versine + cos_angle * lost
        den_imag = retained * sin_angle
        scale_value = numerator / (den_real * den_real + den_imag * den_imag)
        spec_real = spec_real + scale_value * den_real
        spec_imag = spec_imag - scale_value * den_imag
    return (spec_real, spec_imag)


def body(
    query_input, key_input, value_input, short_weight, residue, decay_rate, skip_gain, out_weight
):
    device_index = lax.axis_index("ctx")
    device_count = lax.axis_size("ctx")
    row_count = query_input.shape[0]
    total_rows = row_count * device_count
    tap_count = short_weight.shape[1]
    cut_row = row_count - tap_count + 1
    prior = passed_along(
        (query_input[cut_row:], key_input[cut_row:], value_input[cut_row:]), "ctx", 1
    )
    query_conv = short_filter(query_input, prior[0], short_weight[0])
    key_conv = short_filter(key_input, prior[1], short_weight[1])
    value_conv = short_filter(value_input, prior[2], short_weight[2])
    mixed_input = key_conv * value_conv
    bit_total = device_count.bit_length() - 1
    frequency_row = reversed_index(device_index, bit_total)
    signal_real, signal_imag = forward_spectrum(
        mixed_input, device_index, frequency_row, total_rows
    )
    frequencies = (
        2 * (frequency_row + device_count * jnp.arange(row_count, dtype=jnp.int32))[None, :]
        + jnp.arange(2, dtype=jnp.int32)[:, None]
    )
    filter_real, filter_imag = closed_spectrum(residue, decay_rate, frequencies, total_rows)
    product_real = signal_real * filter_real - signal_imag * filter_imag
    product_imag = signal_real * filter_imag + signal_imag * filter_real
    convolved = inverse_rows(product_real, product_imag, device_index, frequency_row, total_rows)
    gated = (query_conv * (convolved + skip_gain * mixed_input)).astype(jnp.bfloat16)
    partial_value = jnp.dot(gated, out_weight, preferred_element_type=jnp.float32)
    return lax.psum_scatter(
        partial_value.astype(jnp.bfloat16), "ch", scatter_dimension=1, tiled=True
    )


def solution(mesh):
    return jax.shard_map(
        body,
        mesh=mesh,
        in_specs=(
            P("ctx", "ch"),
            P("ctx", "ch"),
            P("ctx", "ch"),
            P(None, None, "ch"),
            P(None, "ch"),
            P(None, "ch"),
            P("ch"),
            P("ch", None),
        ),
        out_specs=P("ctx", "ch"),
        check_vma=False,
    )
```

profile of v0, /device:TPU:32, one launch (start us, length us, event | category | flops | bytes accessed | tf_op | source)
XLA Modules:
  0.0 415.0 jit_solution(10061828376152411717)
XLA Ops:
  7.4 3.4 collective-permute-start.1
  11.7 3.4 collective-permute-start.2
  15.2 0.9 fusion.108
  16.1 1.0 copy.16
  17.1 1.0 copy.18
  18.3 2.4 collective-permute-done.2
  21.7 6.4 %collective-permute-start.3 = (f32[2,128,512]{1,2,0:T(8,128)S(1)}, f32[2,128,512]{1,2,0:T(8,128)S(1)}, u32[]{:S(2)}, u32[]{:S(2)}) collective-permute-start(f32[2,128,512]{1,2,0:T(8,128)S(1)} %pad_maximum_fusion), channel_id=1, source_target_pairs={{0,128},{8,136},{16,144},{24,152},{32,160},{40,168},{48,176},{56,1... | collective-permute-start | bytes 1572872 | tf_op jit(solution)/shard_map/ppermute | solution.py:15
  28.4 30.9 %collective-permute-done.3 = f32[2,128,512]{1,2,0:T(8,128)S(1)} collective-permute-done((f32[2,128,512]{1,2,0:T(8,128)S(1)}, f32[2,128,512]{1,2,0:T(8,128)S(1)}, u32[]{:S(2)}, u32[]{:S(2)}) %collective-permute-start.3) | collective-permute-done | bytes 524320 | tf_op jit(solution)/shard_map/ppermute | solution.py:15
  59.3 13.2 %collective-permute-done.4 = f32[2,128,512]{1,2,0:T(8,128)S(1)} collective-permute-done((f32[2,128,512]{1,2,0:T(8,128)S(1)}, f32[2,128,512]{1,2,0:T(8,128)S(1)}, u32[]{:S(2)}, u32[]{:S(2)}) %collective-permute-start.4) | collective-permute-done | bytes 524320 | tf_op jit(solution)/shard_map/ppermute | solution.py:15
  72.8 2.9 collective-permute-start.6
  75.9 31.1 %collective-permute-done.5 = f32[2,128,512]{1,2,0:T(8,128)S(1)} collective-permute-done((f32[2,128,512]{1,2,0:T(8,128)S(1)}, f32[2,128,512]{1,2,0:T(8,128)S(1)}, u32[]{:S(2)}, u32[]{:S(2)}) %collective-permute-start.5) | collective-permute-done | bytes 524320 | tf_op jit(solution)/shard_map/ppermute | solution.py:15
  107.0 9.7 %collective-permute-done.6 = f32[2,128,512]{1,2,0:T(8,128)S(1)} collective-permute-done((f32[2,128,512]{1,2,0:T(8,128)S(1)}, f32[2,128,512]{1,2,0:T(8,128)S(1)}, u32[]{:S(2)}, u32[]{:S(2)}) %collective-permute-start.6) | collective-permute-done | bytes 524320 | tf_op jit(solution)/shard_map/ppermute | solution.py:15
  117.0 2.8 collective-permute-start.7
  120.2 0.9 multiply_exponential_fusion.3
  121.1 11.4 %collective-permute-done.7 = f32[2,128,512]{1,2,0:T(8,128)S(1)} collective-permute-done((f32[2,128,512]{1,2,0:T(8,128)S(1)}, f32[2,128,512]{1,2,0:T(8,128)S(1)}, u32[]{:S(2)}, u32[]{:S(2)}) %collective-permute-start.7) | collective-permute-done | bytes 524320 | tf_op jit(solution)/shard_map/ppermute | solution.py:15
  132.6 9.5 %collective-permute-done.8 = f32[2,128,512]{1,2,0:T(8,128)S(1)} collective-permute-done((f32[2,128,512]{1,2,0:T(8,128)S(1)}, f32[2,128,512]{1,2,0:T(8,128)S(1)}, u32[]{:S(2)}, u32[]{:S(2)}) %collective-permute-start.8) | collective-permute-done | bytes 524320 | tf_op jit(solution)/shard_map/ppermute | solution.py:15
  142.3 4.5 %collective-permute-start.10 = (f32[2,128,512]{1,2,0:T(8,128)S(1)}, f32[2,128,512]{1,2,0:T(8,128)S(1)}, u32[]{:S(2)}, u32[]{:S(2)}) collective-permute-start(f32[2,128,512]{1,2,0:T(8,128)S(1)} %get-tuple-element.23), channel_id=1, source_target_pairs={{0,16},{8,24},{16,0},{24,8},{32,48},{40,56},{48,32},{56,40},{64,80... | collective-permute-start | bytes 1572872 | tf_op jit(solution)/shard_map/ppermute | solution.py:15
  146.9 1.1 sqrt_multiply_fusion.15
  148.0 1.1 multiply_exponential_fusion.15
  149.1 10.5 %collective-permute-done.10 = f32[2,128,512]{1,2,0:T(8,128)S(1)} collective-permute-done((f32[2,128,512]{1,2,0:T(8,128)S(1)}, f32[2,128,512]{1,2,0:T(8,128)S(1)}, u32[]{:S(2)}, u32[]{:S(2)}) %collective-permute-start.10) | collective-permute-done | bytes 524320 | tf_op jit(solution)/shard_map/ppermute | solution.py:15
  159.6 9.7 %collective-permute-done.9 = f32[2,128,512]{1,2,0:T(8,128)S(1)} collective-permute-done((f32[2,128,512]{1,2,0:T(8,128)S(1)}, f32[2,128,512]{1,2,0:T(8,128)S(1)}, u32[]{:S(2)}, u32[]{:S(2)}) %collective-permute-start.9) | collective-permute-done | bytes 524320 | tf_op jit(solution)/shard_map/ppermute | solution.py:15
  169.5 1.0 collective-permute-start.11
  170.5 1.1 collective-permute-start.12
  171.7 1.0 exponential-minus-one_negate_fusion.15
  172.7 1.1 sqrt_multiply_fusion.14
  173.8 10.6 %collective-permute-done.11 = f32[2,128,512]{1,2,0:T(8,128)S(1)} collective-permute-done((f32[2,128,512]{1,2,0:T(8,128)S(1)}, f32[2,128,512]{1,2,0:T(8,128)S(1)}, u32[]{:S(2)}, u32[]{:S(2)}) %collective-permute-start.11) | collective-permute-done | bytes 524320 | tf_op jit(solution)/shard_map/ppermute | solution.py:15
  184.5 8.7 %collective-permute-done.12 = f32[2,128,512]{1,2,0:T(8,128)S(1)} collective-permute-done((f32[2,128,512]{1,2,0:T(8,128)S(1)}, f32[2,128,512]{1,2,0:T(8,128)S(1)}, u32[]{:S(2)}, u32[]{:S(2)}) %collective-permute-start.12) | collective-permute-done | bytes 524320 | tf_op jit(solution)/shard_map/ppermute | solution.py:15
  195.2 4.8 %multiply_subtract_fusion.1 = (f32[2,128,512]{1,2,0:T(8,128)S(1)}, f32[2,128,512]{1,2,0:T(8,128)S(1)}, f32[2,128,512]{1,2,0:T(8,128)S(1)}, f32[2,128,512]{1,2,0:T(8,128)S(1)}) fusion(f32[2,128,512]{1,2,0:T(8,128)S(1)} %fusion.1, f32[512]{0:T(512)S(1)} %bitcast.147, f32[512]{0:T(512)S(1)} %bitcast.209, f32[512]{0:T(512)S(1)} %bitcast.180, ...), kind=kOutput, calls=%fused_computation.112 | convolution fusion | flops 231473152 | bytes 4396032 | tf_op jit(solution)/shard_map/kb,ebc->ekc/dot_general | solution.py:55
  202.6 1.0 collective-permute-start.13
  203.6 1.1 collective-permute-start.14
  204.9 12.7 %collective-permute-done.13 = f32[2,128,512]{1,2,0:T(8,128)S(1)} collective-permute-done((f32[2,128,512]{1,2,0:T(8,128)S(1)}, f32[2,128,512]{1,2,0:T(8,128)S(1)}, u32[]{:S(2)}, u32[]{:S(2)}) %collective-permute-start.13) | collective-permute-done | bytes 524320 | tf_op jit(solution)/shard_map/ppermute | solution.py:15
  217.6 7.8 %collective-permute-done.14 = f32[2,128,512]{1,2,0:T(8,128)S(1)} collective-permute-done((f32[2,128,512]{1,2,0:T(8,128)S(1)}, f32[2,128,512]{1,2,0:T(8,128)S(1)}, u32[]{:S(2)}, u32[]{:S(2)}) %collective-permute-start.14) | collective-permute-done | bytes 524320 | tf_op jit(solution)/shard_map/ppermute | solution.py:15
  225.7 2.8 collective-permute-start.15
  228.4 0.8 collective-permute-start.16
  229.4 12.7 %collective-permute-done.15 = f32[2,128,512]{1,2,0:T(8,128)S(1)} collective-permute-done((f32[2,128,512]{1,2,0:T(8,128)S(1)}, f32[2,128,512]{1,2,0:T(8,128)S(1)}, u32[]{:S(2)}, u32[]{:S(2)}) %collective-permute-start.15) | collective-permute-done | bytes 524320 | tf_op jit(solution)/shard_map/ppermute | solution.py:15
  242.1 7.9 %collective-permute-done.16 = f32[2,128,512]{1,2,0:T(8,128)S(1)} collective-permute-done((f32[2,128,512]{1,2,0:T(8,128)S(1)}, f32[2,128,512]{1,2,0:T(8,128)S(1)}, u32[]{:S(2)}, u32[]{:S(2)}) %collective-permute-start.16) | collective-permute-done | bytes 524320 | tf_op jit(solution)/shard_map/ppermute | solution.py:15
  250.4 2.0 collective-permute-start.18
  252.6 12.7 %collective-permute-done.17 = f32[2,128,512]{1,2,0:T(8,128)S(1)} collective-permute-done((f32[2,128,512]{1,2,0:T(8,128)S(1)}, f32[2,128,512]{1,2,0:T(8,128)S(1)}, u32[]{:S(2)}, u32[]{:S(2)}) %collective-permute-start.17) | collective-permute-done | bytes 524320 | tf_op jit(solution)/shard_map/ppermute | solution.py:15
  265.2 7.0 %collective-permute-done.18 = f32[2,128,512]{1,2,0:T(8,128)S(1)} collective-permute-done((f32[2,128,512]{1,2,0:T(8,128)S(1)}, f32[2,128,512]{1,2,0:T(8,128)S(1)}, u32[]{:S(2)}, u32[]{:S(2)}) %collective-permute-start.18) | collective-permute-done | bytes 524320 | tf_op jit(solution)/shard_map/ppermute | solution.py:15
  272.5 4.2 %collective-permute-start.19 = (f32[2,128,512]{1,2,0:T(8,128)S(1)}, f32[2,128,512]{1,2,0:T(8,128)S(1)}, u32[]{:S(2)}, u32[]{:S(2)}) collective-permute-start(f32[2,128,512]{1,2,0:T(8,128)S(1)} %get-tuple-element.13), channel_id=1, source_target_pairs={{0,64},{8,72},{16,80},{24,88},{32,96},{40,104},{48,112},{56,120},{... | collective-permute-start | bytes 1572872 | tf_op jit(solution)/shard_map/ppermute | solution.py:15
  277.0 29.4 %collective-permute-done.19 = f32[2,128,512]{1,2,0:T(8,128)S(1)} collective-permute-done((f32[2,128,512]{1,2,0:T(8,128)S(1)}, f32[2,128,512]{1,2,0:T(8,128)S(1)}, u32[]{:S(2)}, u32[]{:S(2)}) %collective-permute-start.19) | collective-permute-done | bytes 524320 | tf_op jit(solution)/shard_map/ppermute | solution.py:15
  306.4 10.5 %collective-permute-done.20 = f32[2,128,512]{1,2,0:T(8,128)S(1)} collective-permute-done((f32[2,128,512]{1,2,0:T(8,128)S(1)}, f32[2,128,512]{1,2,0:T(8,128)S(1)}, u32[]{:S(2)}, u32[]{:S(2)}) %collective-permute-start.20) | collective-permute-done | bytes 524320 | tf_op jit(solution)/shard_map/ppermute | solution.py:15
  317.1 3.2 collective-permute-start.21
  320.2 2.9 collective-permute-start.22
  323.3 1.9 collective-permute-start
  325.4 39.6 %collective-permute-done = bf16[2,512]{0,1:T(8,128)(2,1)S(1)} collective-permute-done((bf16[2,512]{0,1:T(8,128)(2,1)S(1)}, bf16[2,512]{0,1:T(8,128)(2,1)S(1)}, u32[]{:S(2)}, u32[]{:S(2)}) %collective-permute-start) | collective-permute-done | bytes 2080 | tf_op jit(solution)/shard_map/ppermute | solution.py:21
  365.2 6.4 %convolution_convert_fusion = bf16[128,8192]{1,0:T(8,128)(2,1)} fusion(bf16[512,8192]{1,0:T(8,128)(2,1)} %param.19, f32[2,128,512]{1,2,0:T(8,128)S(1)} %add_select_fusion.2, f32[130,512]{0,1:T(8,128)S(1)} %maximum_convert_fusion, f32[128,512]{0,1:T(8,128)S(1)} %get-tuple-element.9, f32[2,128,512]{1,2,0:T(8,128)S(1)} %get-tuple-element.10, ...), kind=kOutput, calls=%fused_computation | convolution fusion | flops 1075904512 | bytes 12592129 | tf_op jit(solution)/shard_map/dot_general | solution.py:186
  371.7 36.5 %reduce-scatter.2.cloned.1.call-done = bf16[128,1024]{1,0:T(8,128)(2,1)} async-done(((bf16[128,8192]{1,0:T(8,128)(2,1)}), bf16[128,1024]{1,0:T(8,128)(2,1)}) %reduce-scatter.2.cloned.1.call-update) | async-done | bytes 262160 | tf_op jit(solution)/shard_map/reduce_scatter | solution.py:187
  (61 shorter events, 10.7 us)
Async XLA Ops:
  6.5 401.6 %reduce-scatter.2.cloned.1.call-start = ((), (), s32[]{:S(2)}) async-start(), calls=%async_computation.1 | async-start | bytes 2359296 | tf_op jit(solution)/shard_map/reduce_scatter | solution.py:187
  7.4 10.7 %collective-permute-start.1 = (bf16[2,512]{0,1:T(8,128)(2,1)S(1)}, bf16[2,512]{0,1:T(8,128)(2,1)S(1)}, u32[]{:S(2)}, u32[]{:S(2)}) collective-permute-start(bf16[2,512]{0,1:T(8,128)(2,1)S(1)} %copy.15), channel_id=1, source_target_pairs={{0,8},{8,16},{16,24},{24,32},{32,40},{40,48},{48,56},{56,64},{64,7... | collective-permute-start | bytes 6152 | tf_op jit(solution)/shard_map/ppermute | solution.py:21
  11.7 9.0 %collective-permute-start.2 = (bf16[2,512]{0,1:T(8,128)(2,1)S(1)}, bf16[2,512]{0,1:T(8,128)(2,1)S(1)}, u32[]{:S(2)}, u32[]{:S(2)}) collective-permute-start(bf16[2,512]{0,1:T(8,128)(2,1)S(1)} %copy.17), channel_id=1, source_target_pairs={{0,8},{8,16},{16,24},{24,32},{32,40},{40,48},{48,56},{56,64},{64,7... | collective-permute-start | bytes 6152 | tf_op jit(solution)/shard_map/ppermute | solution.py:21
  21.7 37.6 %collective-permute-start.3 = (f32[2,128,512]{1,2,0:T(8,128)S(1)}, f32[2,128,512]{1,2,0:T(8,128)S(1)}, u32[]{:S(2)}, u32[]{:S(2)}) collective-permute-start(f32[2,128,512]{1,2,0:T(8,128)S(1)} %pad_maximum_fusion), channel_id=1, source_target_pairs={{0,128},{8,136},{16,144},{24,152},{32,160},{40,168},{48,176},{56,1... | collective-permute-start | bytes 1572872 | tf_op jit(solution)/shard_map/ppermute | solution.py:15
  28.1 165.3 %copy-start.2 = (f32[128,128,1]{1,0,2:T(8,128)S(1)}, f32[128,128,1]{1,0,2:T(8,128)}, u32[]{:S(2)}) copy-start(f32[128,128,1]{1,0,2:T(8,128)} %constant.165) | copy-start | bytes 196612
  28.1 44.4 %collective-permute-start.4 = (f32[2,128,512]{1,2,0:T(8,128)S(1)}, f32[2,128,512]{1,2,0:T(8,128)S(1)}, u32[]{:S(2)}, u32[]{:S(2)}) collective-permute-start(f32[2,128,512]{1,2,0:T(8,128)S(1)} %stack.19), channel_id=1, source_target_pairs={{0,128},{8,136},{16,144},{24,152},{32,160},{40,168},{48,176},{56,1... | collective-permute-start | bytes 1572872 | tf_op jit(solution)/shard_map/ppermute | solution.py:15
  72.7 121.9 %copy-start = (f32[128,128,1]{1,0,2:T(8,128)S(1)}, f32[128,128,1]{1,0,2:T(8,128)}, u32[]{:S(2)}) copy-start(f32[128,128,1]{1,0,2:T(8,128)} %constant.164) | copy-start | bytes 196612
  72.7 34.3 %collective-permute-start.5 = (f32[2,128,512]{1,2,0:T(8,128)S(1)}, f32[2,128,512]{1,2,0:T(8,128)S(1)}, u32[]{:S(2)}, u32[]{:S(2)}) collective-permute-start(f32[2,128,512]{1,2,0:T(8,128)S(1)} %get-tuple-element.26), channel_id=1, source_target_pairs={{0,64},{8,72},{16,80},{24,88},{32,96},{40,104},{48,112},{56,120},{... | collective-permute-start | bytes 1572872 | tf_op jit(solution)/shard_map/ppermute | solution.py:15
  72.8 43.9 %collective-permute-start.6 = (f32[2,128,512]{1,2,0:T(8,128)S(1)}, f32[2,128,512]{1,2,0:T(8,128)S(1)}, u32[]{:S(2)}, u32[]{:S(2)}) collective-permute-start(f32[2,128,512]{1,2,0:T(8,128)S(1)} %get-tuple-element.27), channel_id=1, source_target_pairs={{0,64},{8,72},{16,80},{24,88},{32,96},{40,104},{48,112},{56,120},{... | collective-permute-start | bytes 1572872 | tf_op jit(solution)/shard_map/ppermute | solution.py:15
  117.0 15.6 %collective-permute-start.7 = (f32[2,128,512]{1,2,0:T(8,128)S(1)}, f32[2,128,512]{1,2,0:T(8,128)S(1)}, u32[]{:S(2)}, u32[]{:S(2)}) collective-permute-start(f32[2,128,512]{1,2,0:T(8,128)S(1)} %get-tuple-element.24), channel_id=1, source_target_pairs={{0,32},{8,40},{16,48},{24,56},{32,0},{40,8},{48,16},{56,24},{64,96... | collective-permute-start | bytes 1572872 | tf_op jit(solution)/shard_map/ppermute | solution.py:15
  119.7 22.4 %collective-permute-start.8 = (f32[2,128,512]{1,2,0:T(8,128)S(1)}, f32[2,128,512]{1,2,0:T(8,128)S(1)}, u32[]{:S(2)}, u32[]{:S(2)}) collective-permute-start(f32[2,128,512]{1,2,0:T(8,128)S(1)} %get-tuple-element.25), channel_id=1, source_target_pairs={{0,32},{8,40},{16,48},{24,56},{32,0},{40,8},{48,16},{56,24},{64,96... | collective-permute-start | bytes 1572872 | tf_op jit(solution)/shard_map/ppermute | solution.py:15
  142.3 17.3 %collective-permute-start.10 = (f32[2,128,512]{1,2,0:T(8,128)S(1)}, f32[2,128,512]{1,2,0:T(8,128)S(1)}, u32[]{:S(2)}, u32[]{:S(2)}) collective-permute-start(f32[2,128,512]{1,2,0:T(8,128)S(1)} %get-tuple-element.23), channel_id=1, source_target_pairs={{0,16},{8,24},{16,0},{24,8},{32,48},{40,56},{48,32},{56,40},{64,80... | collective-permute-start | bytes 1572872 | tf_op jit(solution)/shard_map/ppermute | solution.py:15
  146.8 22.5 %collective-permute-start.9 = (f32[2,128,512]{1,2,0:T(8,128)S(1)}, f32[2,128,512]{1,2,0:T(8,128)S(1)}, u32[]{:S(2)}, u32[]{:S(2)}) collective-permute-start(f32[2,128,512]{1,2,0:T(8,128)S(1)} %get-tuple-element.22), channel_id=1, source_target_pairs={{0,16},{8,24},{16,0},{24,8},{32,48},{40,56},{48,32},{56,40},{64,80... | collective-permute-start | bytes 1572872 | tf_op jit(solution)/shard_map/ppermute | solution.py:15
  169.5 14.9 %collective-permute-start.11 = (f32[2,128,512]{1,2,0:T(8,128)S(1)}, f32[2,128,512]{1,2,0:T(8,128)S(1)}, u32[]{:S(2)}, u32[]{:S(2)}) collective-permute-start(f32[2,128,512]{1,2,0:T(8,128)S(1)} %get-tuple-element.20), channel_id=1, source_target_pairs={{0,8},{8,0},{16,24},{24,16},{32,40},{40,32},{48,56},{56,48},{64,72... | collective-permute-start | bytes 1572872 | tf_op jit(solution)/shard_map/ppermute | solution.py:15
  170.5 22.7 %collective-permute-start.12 = (f32[2,128,512]{1,2,0:T(8,128)S(1)}, f32[2,128,512]{1,2,0:T(8,128)S(1)}, u32[]{:S(2)}, u32[]{:S(2)}) collective-permute-start(f32[2,128,512]{1,2,0:T(8,128)S(1)} %get-tuple-element.21), channel_id=1, source_target_pairs={{0,8},{8,0},{16,24},{24,16},{32,40},{40,32},{48,56},{56,48},{64,72... | collective-permute-start | bytes 1572872 | tf_op jit(solution)/shard_map/ppermute | solution.py:15
  195.2 6.1 %copy-start.1 = (f32[128,128,1]{1,0,2:T(8,128)S(1)}, f32[128,128,1]{1,0,2:T(8,128)}, u32[]{:S(2)}) copy-start(f32[128,128,1]{1,0,2:T(8,128)} %constant.166) | copy-start | bytes 196612
  201.3 121.8 %copy-start.3 = (bf16[128,512]{1,0:T(8,128)(2,1)S(1)}, bf16[128,512]{1,0:T(8,128)(2,1)}, u32[]{:S(2)}) copy-start(bf16[128,512]{1,0:T(8,128)(2,1)} %param.12) | copy-start | bytes 393220
  201.9 163.4 %copy-start.4 = (f32[512]{0:T(512)S(1)}, f32[512]{0:T(512)}, u32[]{:S(2)}) copy-start(f32[512]{0:T(512)} %param.18) | copy-start | bytes 6148
  202.6 14.9 %collective-permute-start.13 = (f32[2,128,512]{1,2,0:T(8,128)S(1)}, f32[2,128,512]{1,2,0:T(8,128)S(1)}, u32[]{:S(2)}, u32[]{:S(2)}) collective-permute-start(f32[2,128,512]{1,2,0:T(8,128)S(1)} %get-tuple-element.29), channel_id=1, source_target_pairs={{0,8},{8,0},{16,24},{24,16},{32,40},{40,32},{48,56},{56,48},{64,72... | collective-permute-start | bytes 1572872 | tf_op jit(solution)/shard_map/ppermute | solution.py:15
  203.6 21.8 %collective-permute-start.14 = (f32[2,128,512]{1,2,0:T(8,128)S(1)}, f32[2,128,512]{1,2,0:T(8,128)S(1)}, u32[]{:S(2)}, u32[]{:S(2)}) collective-permute-start(f32[2,128,512]{1,2,0:T(8,128)S(1)} %get-tuple-element.28), channel_id=1, source_target_pairs={{0,8},{8,0},{16,24},{24,16},{32,40},{40,32},{48,56},{56,48},{64,72... | collective-permute-start | bytes 1572872 | tf_op jit(solution)/shard_map/ppermute | solution.py:15
  225.7 16.5 %collective-permute-start.15 = (f32[2,128,512]{1,2,0:T(8,128)S(1)}, f32[2,128,512]{1,2,0:T(8,128)S(1)}, u32[]{:S(2)}, u32[]{:S(2)}) collective-permute-start(f32[2,128,512]{1,2,0:T(8,128)S(1)} %get-tuple-element.17), channel_id=1, source_target_pairs={{0,16},{8,24},{16,0},{24,8},{32,48},{40,56},{48,32},{56,40},{64,80... | collective-permute-start | bytes 1572872 | tf_op jit(solution)/shard_map/ppermute | solution.py:15
  228.4 21.6 %collective-permute-start.16 = (f32[2,128,512]{1,2,0:T(8,128)S(1)}, f32[2,128,512]{1,2,0:T(8,128)S(1)}, u32[]{:S(2)}, u32[]{:S(2)}) collective-permute-start(f32[2,128,512]{1,2,0:T(8,128)S(1)} %get-tuple-element.16), channel_id=1, source_target_pairs={{0,16},{8,24},{16,0},{24,8},{32,48},{40,56},{48,32},{56,40},{64,80... | collective-permute-start | bytes 1572872 | tf_op jit(solution)/shard_map/ppermute | solution.py:15
  250.3 14.9 %collective-permute-start.17 = (f32[2,128,512]{1,2,0:T(8,128)S(1)}, f32[2,128,512]{1,2,0:T(8,128)S(1)}, u32[]{:S(2)}, u32[]{:S(2)}) collective-permute-start(f32[2,128,512]{1,2,0:T(8,128)S(1)} %get-tuple-element.15), channel_id=1, source_target_pairs={{0,32},{8,40},{16,48},{24,56},{32,0},{40,8},{48,16},{56,24},{64,96... | collective-permute-start | bytes 1572872 | tf_op jit(solution)/shard_map/ppermute | solution.py:15
  250.4 21.8 %collective-permute-start.18 = (f32[2,128,512]{1,2,0:T(8,128)S(1)}, f32[2,128,512]{1,2,0:T(8,128)S(1)}, u32[]{:S(2)}, u32[]{:S(2)}) collective-permute-start(f32[2,128,512]{1,2,0:T(8,128)S(1)} %get-tuple-element.14), channel_id=1, source_target_pairs={{0,32},{8,40},{16,48},{24,56},{32,0},{40,8},{48,16},{56,24},{64,96... | collective-permute-start | bytes 1572872 | tf_op jit(solution)/shard_map/ppermute | solution.py:15
  272.5 33.9 %collective-permute-start.19 = (f32[2,128,512]{1,2,0:T(8,128)S(1)}, f32[2,128,512]{1,2,0:T(8,128)S(1)}, u32[]{:S(2)}, u32[]{:S(2)}) collective-permute-start(f32[2,128,512]{1,2,0:T(8,128)S(1)} %get-tuple-element.13), channel_id=1, source_target_pairs={{0,64},{8,72},{16,80},{24,88},{32,96},{40,104},{48,112},{56,120},{... | collective-permute-start | bytes 1572872 | tf_op jit(solution)/shard_map/ppermute | solution.py:15
  276.7 40.1 %collective-permute-start.20 = (f32[2,128,512]{1,2,0:T(8,128)S(1)}, f32[2,128,512]{1,2,0:T(8,128)S(1)}, u32[]{:S(2)}, u32[]{:S(2)}) collective-permute-start(f32[2,128,512]{1,2,0:T(8,128)S(1)} %get-tuple-element.12), channel_id=1, source_target_pairs={{0,64},{8,72},{16,80},{24,88},{32,96},{40,104},{48,112},{56,120},{... | collective-permute-start | bytes 1572872 | tf_op jit(solution)/shard_map/ppermute | solution.py:15
  317.1 48.1 %collective-permute-start.21 = (f32[2,128,512]{1,2,0:T(8,128)S(1)}, f32[2,128,512]{1,2,0:T(8,128)S(1)}, u32[]{:S(2)}, u32[]{:S(2)}) collective-permute-start(f32[2,128,512]{1,2,0:T(8,128)S(1)} %get-tuple-element.11), channel_id=1, source_target_pairs={{0,128},{8,136},{16,144},{24,152},{32,160},{40,168},{48,176},{56,1... | collective-permute-start | bytes 1572872 | tf_op jit(solution)/shard_map/ppermute | solution.py:15
  320.2 45.0 %collective-permute-start.22 = (f32[2,128,512]{1,2,0:T(8,128)S(1)}, f32[2,128,512]{1,2,0:T(8,128)S(1)}, u32[]{:S(2)}, u32[]{:S(2)}) collective-permute-start(f32[2,128,512]{1,2,0:T(8,128)S(1)} %get-tuple-element.10), channel_id=1, source_target_pairs={{0,128},{8,136},{16,144},{24,152},{32,160},{40,168},{48,176},{56,1... | collective-permute-start | bytes 1572872 | tf_op jit(solution)/shard_map/ppermute | solution.py:15
  323.3 41.7 %collective-permute-start = (bf16[2,512]{0,1:T(8,128)(2,1)S(1)}, bf16[2,512]{0,1:T(8,128)(2,1)S(1)}, u32[]{:S(2)}, u32[]{:S(2)}) collective-permute-start(bf16[2,512]{0,1:T(8,128)(2,1)S(1)} %copy.13), channel_id=1, source_target_pairs={{0,8},{8,16},{16,24},{24,32},{32,40},{40,48},{48,56},{56,64},{64,7... | collective-permute-start | bytes 6152 | tf_op jit(solution)/shard_map/ppermute | solution.py:21
Sparse Core Ops, SparseCore 0:
  371.8 36.3 reduce-scatter.1
where the time goes:
time: 416 us; the launch traced here: 415 us
  waiting for transfers between devices  325 us (78%)
  starting transfers between devices  46 us (11%)
  matrix products  15.4 us (4%)
  between operations  15.1 us (4%)
  other arithmetic  8.9 us (2%)
  local copies, waits for them, and re-layouts  5.08 us (1%)
    ppermute x20, waiting for transfers between devices, swapped(): return lax.ppermute(value, axis, pairs)  246 us
    ppermute x3, waiting for transfers between devices, passed_along(): return lax.ppermute(block, axis, route)  42 us
    ppermute x20, starting transfers between devices, swapped(): return lax.ppermute(value, axis, pairs)  37.2 us
    reduce_scatter x1, waiting for transfers between devices, body(): lax.psum_scatter(partial_value.astype(jnp.bfloat16), 'ch', scatter_dimens...  36.5 us
    ppermute x3, starting transfers between devices, passed_along(): return lax.ppermute(block, axis, route)  8.72 us
  transfers between devices with their start and end apart: 24, of which 21 were waited for; matrix products, arithmetic and copies ran while one was open for 2% of the time, Pallas kernels for 0%

commit v1 on v0

v1 whole, which is shorter than its diff:
```python
import functools

import jax
import jax.numpy as jnp
from jax import lax
from jax.experimental import pallas as pl
from jax.experimental.pallas import tpu as pltpu
from jax.sharding import PartitionSpec as P

F32 = jnp.float32
BF16 = jnp.bfloat16
SUBLANES = 8
LANES = 128


def rows_of(shape):
    return lax.broadcasted_iota(jnp.int32, shape, 0)


def short_conv(raw, prior, taps):
    x = raw.astype(F32)
    row = rows_of(x.shape)
    older = prior[0:1].astype(F32)
    newer = prior[1:2].astype(F32)
    back1 = jnp.where(row == 0, newer, pltpu.roll(x, 1, axis=0))
    back2 = jnp.where(
        row == 0, older, jnp.where(row == 1, newer, pltpu.roll(x, 2, axis=0))
    )
    return taps[0:1] * x + taps[1:2] * back1 + taps[2:3] * back2


def spread(row):
    return jnp.broadcast_to(row, (SUBLANES, row.shape[-1]))


def state_kernel(k_ref, v_ref, halo_ref, taps_ref, rate_ref, state_ref, ends_ref, mixed):
    modes, width = rate_ref.shape
    steps = k_ref.shape[0] // SUBLANES
    product = short_conv(k_ref[...], halo_ref[0:2], taps_ref[1]) * short_conv(
        v_ref[...], halo_ref[2:4], taps_ref[2]
    )
    for at in range(0, width, LANES):
        mixed[at // LANES] = product[:, at : at + LANES]
    left = (SUBLANES - 1 - rows_of((SUBLANES, LANES))).astype(F32) * float(steps)
    for at in range(0, width, LANES):
        cols = pl.ds(at, LANES)
        rate = rate_ref[:, cols]
        decay = jnp.exp(-rate)
        keep = [spread(decay[r : r + 1]) for r in range(modes)]
        held = [mixed[at // LANES, pl.ds(0, SUBLANES, steps), :]] * modes
        for a in range(1, steps):
            fresh = mixed[at // LANES, pl.ds(a, SUBLANES, steps), :]
            held = [keep[r] * held[r] + fresh for r in range(modes)]
        totals = []
        for r in range(modes):
            ends_ref[r, :, cols] = held[r]
            weight = jnp.exp(-spread(rate[r : r + 1]) * left)
            totals.append(jnp.sum(weight * held[r], axis=0, keepdims=True))
        state_ref[:, cols] = jnp.concatenate(totals, axis=0).astype(state_ref.dtype)


def gate_kernel(
    ctx_ref, q_ref, k_ref, v_ref, halo_ref, taps_ref, residue_ref, rate_ref, skip_ref,
    states_ref, ends_ref, gated_ref, mixed, carry, convolved,
):
    modes, width = rate_ref.shape
    rows = k_ref.shape[0]
    steps = rows // SUBLANES
    product = short_conv(k_ref[...], halo_ref[0:2], taps_ref[1]) * short_conv(
        v_ref[...], halo_ref[2:4], taps_ref[2]
    )
    for at in range(0, width, LANES):
        mixed[at // LANES] = product[:, at : at + LANES]
    across = jnp.exp(-rate_ref[...] * float(rows))

    def add_block(j, total):
        return across * total + states_ref[j].astype(F32)

    carry[...] = lax.fori_loop(0, ctx_ref[0], add_block, jnp.zeros((modes, width), F32))
    seg = rows_of((SUBLANES, LANES))
    for at in range(0, width, LANES):
        cols = pl.ds(at, LANES)
        rate = rate_ref[:, cols]
        decay = jnp.exp(-rate)
        skip1 = jnp.exp(-rate * float(steps))
        skip2 = skip1 * skip1
        skip4 = skip2 * skip2
        gain = residue_ref[:, cols] * jnp.sqrt(2.0 * rate)
        begin = carry[:, cols]
        held = []
        for r in range(modes):
            one = slice(r, r + 1)
            h = jnp.where(seg == 0, spread(begin[one]), pltpu.roll(ends_ref[r, :, cols], 1, axis=0))
            for apart, factor in ((1, skip1), (2, skip2), (4, skip4)):
                h = h + jnp.where(seg >= apart, spread(factor[one]), 0.0) * pltpu.roll(h, apart, axis=0)
            held.append(h)
        keep = [spread(decay[r : r + 1]) for r in range(modes)]
        gains = [spread(gain[r : r + 1]) for r in range(modes)]
        for a in range(steps):
            picked = pl.ds(a, SUBLANES, steps)
            fresh = mixed[at // LANES, picked, :]
            held = [keep[r] * held[r] + fresh for r in range(modes)]
            terms = [gains[r] * held[r] for r in range(modes)]
            while len(terms) > 1:
                terms = [x + y for x, y in zip(terms[::2], terms[1::2])]
            convolved[at // LANES, picked, :] = terms[0]
    query = short_conv(q_ref[...], halo_ref[4:6], taps_ref[0])
    for at in range(0, width, LANES):
        cols = pl.ds(at, LANES)
        long = convolved[at // LANES] + skip_ref[:, cols] * mixed[at // LANES]
        gated_ref[:, cols] = (query[:, at : at + LANES] * long).astype(gated_ref.dtype)


def project_kernel(order_ref, gated_ref, weight_ref, out_ref):
    out_ref[...] = jnp.dot(gated_ref[...], weight_ref[...], preferred_element_type=F32).astype(
        out_ref.dtype
    )


def project_add_kernel(order_ref, gated_ref, weight_ref, other_ref, out_ref):
    out_ref[...] = (
        jnp.dot(gated_ref[...], weight_ref[...], preferred_element_type=F32)
        + other_ref[...].astype(F32)
    ).astype(out_ref.dtype)


def project(order, gated, weight, width, other=None, dtype=BF16):
    rows, depth = gated.shape
    count = order.shape[0]
    specs = [
        pl.BlockSpec((rows, depth), lambda i, o: (0, 0)),
        pl.BlockSpec((depth, width), lambda i, o: (0, o[i])),
    ]
    operands = [order, gated, weight]
    if other is not None:
        specs.append(pl.BlockSpec((rows, width), lambda i, o: (i, 0)))
        operands.append(other)
    return pl.pallas_call(
        project_kernel if other is None else project_add_kernel,
        out_shape=jax.ShapeDtypeStruct((count * rows, width), dtype),
        grid_spec=pltpu.PrefetchScalarGridSpec(
            num_scalar_prefetch=1,
            grid=(count,),
            in_specs=specs,
            out_specs=pl.BlockSpec((rows, width), lambda i, o: (i, 0)),
        ),
        cost_estimate=pl.CostEstimate(
            flops=2 * rows * depth * width * count,
            bytes_accessed=2 * count * width * (depth + rows),
            transcendentals=0,
        ),
    )(*operands)


def body(
    query_input, key_input, value_input, short_weight, residue, decay_rate, skip_gain, out_weight
):
    ctx = lax.axis_index("ctx")
    blocks = lax.axis_size("ctx")
    ch = lax.axis_index("ch")
    parts = lax.axis_size("ch")
    chips = parts // 2
    rows, width = query_input.shape
    modes = residue.shape[0]
    last = rows - (short_weight.shape[1] - 1)
    edge = jnp.concatenate(
        [key_input[last:], value_input[last:], query_input[last:], query_input[last:]], axis=0
    )
    halo = lax.ppermute(edge, "ctx", [(i, i + 1) for i in range(blocks - 1)])

    whole = pl.BlockSpec(memory_space=pltpu.VMEM)
    state, ends = pl.pallas_call(
        state_kernel,
        out_shape=(
            jax.ShapeDtypeStruct((modes, width), BF16),
            jax.ShapeDtypeStruct((modes, SUBLANES, width), F32),
        ),
        in_specs=[whole] * 5,
        out_specs=(whole, whole),
        scratch_shapes=[pltpu.VMEM((width // LANES, rows, LANES), F32)],
    )(key_input, value_input, halo, short_weight, decay_rate)

    states = lax.all_to_all(
        jnp.broadcast_to(state[None], (blocks, modes, width)), "ctx", 0, 0
    )

    gated = pl.pallas_call(
        gate_kernel,
        out_shape=jax.ShapeDtypeStruct((rows, width), BF16),
        in_specs=[pl.BlockSpec(memory_space=pltpu.SMEM)] + [whole] * 10,
        out_specs=whole,
        scratch_shapes=[
            pltpu.VMEM((width // LANES, rows, LANES), F32),
            pltpu.VMEM((modes, width), F32),
            pltpu.VMEM((width // LANES, rows, LANES), F32),
        ],
    )(
        ctx[None].astype(jnp.int32), query_input, key_input, value_input, halo, short_weight,
        residue, decay_rate, skip_gain[None], states, ends,
    )

    columns = out_weight.shape[1] // parts
    core_swap = [(i, i ^ 1) for i in range(parts)]

    def along_y(apart):
        return [(i, (i + 2 * apart) % parts) for i in range(parts)]

    def blocks_for(offsets, core):
        return (ch // 2 + jnp.array(offsets, jnp.int32)) % chips * 2 + core

    mine, partner = ch % 2, 1 - ch % 2
    sent_a = project(blocks_for((2, 1), partner), gated, out_weight, columns)
    got_a = lax.ppermute(sent_a, "ch", core_swap)
    sent_b = project(blocks_for((3, 0), partner), gated, out_weight, columns)
    got_b = lax.ppermute(sent_b, "ch", core_swap)
    far = project(blocks_for((2, 1), mine), gated, out_weight, columns, got_a)
    from2 = lax.ppermute(far[:rows], "ch", along_y(2))
    from1 = lax.ppermute(far[rows:], "ch", along_y(1))
    near = project(blocks_for((3, 0), mine), gated, out_weight, columns, got_b, F32)
    from3 = lax.ppermute(near[:rows].astype(BF16), "ch", along_y(3))
    total = (
        near[rows:] + from1.astype(F32) + from2.astype(F32) + from3.astype(F32)
    )
    return total.astype(BF16)


def solution(mesh):
    return jax.shard_map(
        body,
        mesh=mesh,
        in_specs=(
            P("ctx", "ch"),
            P("ctx", "ch"),
            P("ctx", "ch"),
            P(None, None, "ch"),
            P(None, "ch"),
            P(None, "ch"),
            P("ch"),
            P("ch", None),
        ),
        out_specs=P("ctx", "ch"),
        check_vma=False,
    )
```

time: 416 us -> 78.5 us (0.19)
  waiting for transfers between devices: 325 us -> 25.4 us
  starting transfers between devices: 46 us -> 19.8 us
  Pallas kernels: 0 us -> 19.2 us
  matrix products: 15.4 us -> 0 us
  between operations: 15.1 us -> 0.07 us
  other arithmetic: 8.9 us -> 4.28 us
    ppermute x23 -> x6, waiting for transfers between devices: 288 us -> 10.6 us  [the longest x1 4.95 us: body(): from2 = lax.ppermute(far[:rows], 'ch', along_y(2))]
    reduce_scatter x1 -> x0, waiting for transfers between devices: 36.5 us -> none  [body(): lax.psum_scatter(partial_value.astype(jnp.bfloat16), 'ch', scatter_dimens...]
    ppermute x23 -> x6, starting transfers between devices: 46 us -> 9.89 us  [the longest x1 3.4 us: body(): halo = lax.ppermute(edge, 'ctx', [(i, i + 1) for i in range(blocks - 1)])]
    pallas_call x0 -> x6, Pallas kernels: none -> 19.2 us  [the longest x4 13.5 us: project(): pl.pallas_call(project_kernel if other is None else project_add_kernel, o...]
    dot_general x9 -> x0, matrix products: 15.4 us -> none  [the longest x1 6.4 us: body(): jnp.dot(gated, out_weight, preferred_element_type=jnp.float32)]
    all_to_all x0 -> x1, waiting for transfers between devices: none -> 14.8 us  [body(): lax.all_to_all(jnp.broadcast_to(state[None], (blocks, modes, width)), 'ct...]
    all_to_all x0 -> x1, starting transfers between devices: none -> 9.94 us  [body(): lax.all_to_all(jnp.broadcast_to(state[None], (blocks, modes, width)), 'ct...]
  transfers between devices with their start and end apart: 24 -> 7, of which waited for: 21 -> 4; matrix products, arithmetic and copies ran while one was open for 2% -> 6% of each run, Pallas kernels for 0% -> 13%
where the time goes in v1:
time: 78.5 us; the launch traced here: 77.5 us
  waiting for transfers between devices  25.4 us (32%)
  starting transfers between devices  19.8 us (25%)
  Pallas kernels  19.2 us (24%)
  local copies, waits for them, and re-layouts  8.82 us (11%)
  other arithmetic  4.28 us (5%)
    all_to_all x1, waiting for transfers between devices, body(): lax.all_to_all(jnp.broadcast_to(state[None], (blocks, modes, width)), 'ct...  14.8 us
    pallas_call x4, Pallas kernels, project(): pl.pallas_call(project_kernel if other is None else project_add_kernel, o...  13.5 us
    all_to_all x1, starting transfers between devices, body(): lax.all_to_all(jnp.broadcast_to(state[None], (blocks, modes, width)), 'ct...  9.94 us
    ppermute x1, waiting for transfers between devices, body(): from2 = lax.ppermute(far[:rows], 'ch', along_y(2))  4.95 us
    ppermute x1, waiting for transfers between devices, body(): halo = lax.ppermute(edge, 'ctx', [(i, i + 1) for i in range(blocks - 1)])  4.25 us
    ppermute x1, starting transfers between devices, body(): halo = lax.ppermute(edge, 'ctx', [(i, i + 1) for i in range(blocks - 1)])  3.4 us
    pallas_call x1, Pallas kernels, body(): pl.pallas_call(gate_kernel, out_shape=jax.ShapeDtypeStruct((rows, width),...  3.25 us
    unnamed x8, local copies, waits for them, and re-layouts  3.02 us
  transfers between devices with their start and end apart: 7, of which 4 were waited for; matrix products, arithmetic and copies ran while one was open for 6% of the time, Pallas kernels for 13%

profile of v1, /device:TPU:32, one launch (start us, length us, event | category | flops | bytes accessed | tf_op | source)
XLA Modules:
  0.0 77.5 jit_solution(10946945290087182681)
XLA Ops:
  0.0 0.7 slice.23
  0.7 0.7 slice.24
  1.4 0.7 slice.25
  2.1 3.4 %collective-permute-start = (bf16[8,512]{1,0:T(8,128)(2,1)S(1)}, bf16[8,512]{1,0:T(8,128)(2,1)S(1)}, u32[]{:S(2)}, u32[]{:S(2)}) collective-permute-start(bf16[8,512]{1,0:T(8,128)(2,1)S(1)} %pad_maximum_fusion), channel_id=1, source_target_pairs={{0,8},{8,16},{16,24},{24,32},{32,40},{40,48},{48,56},{56,64},{64,7... | collective-permute-start | bytes 24584 | tf_op jit(solution)/shard_map/ppermute | solution.py:169
  5.5 4.2 %collective-permute-done.halo_ref = bf16[8,512]{1,0:T(8,128)(2,1)S(1)} collective-permute-done((bf16[8,512]{1,0:T(8,128)(2,1)S(1)}, bf16[8,512]{1,0:T(8,128)(2,1)S(1)}, u32[]{:S(2)}, u32[]{:S(2)}) %collective-permute-start) | collective-permute-done | bytes 8224 | tf_op jit(solution)/shard_map/ppermute | solution.py:169
  9.8 0.0 copy-start.3
  9.8 0.6 copy-done.3
  10.4 2.4 %shard_map.118 = (bf16[16,512]{1,0:T(8,128)(2,1)}, f32[16,8,512]{2,1,0:T(8,128)}) custom-call(bf16[128,512]{1,0:T(8,128)(2,1)} %k_ref.3, bf16[128,512]{1,0:T(8,128)(2,1)} %v_ref.3, bf16[8,512]{1,0:T(8,128)(2,1)} %copy-done.3, f32[3,3,512]{2,1,0:T(4,128)} %taps_ref.3, f32[16,512]{1,0:T(8,128)} %rate_ref.3), custom_call_target="tpu_custom_call" | custom-call | tf_op jit(solution)/shard_map/pallas_call | solution.py:172
  12.7 1.6 %broadcast_in_dim.14 = bf16[32,16,512]{2,1,0:T(8,128)(2,1)} broadcast(bf16[16,512]{1,0:T(8,128)(2,1)} %get-tuple-element.7), dimensions={1,2} | broadcast | bytes 540672 | tf_op jit(solution)/shard_map/broadcast_in_dim | solution.py:184
  14.3 9.9 %all-to-all-start = ((bf16[32,16,512]{2,1,0:T(8,128)(2,1)}), bf16[32,16,512]{2,1,0:T(8,128)(2,1)S(1)}, u32[]{:S(2)}, u32[]{:S(2)}) async-start(bf16[32,16,512]{2,1,0:T(8,128)(2,1)} %broadcast_in_dim.14), calls=%async_computation | async-start | bytes 1048576 | tf_op jit(solution)/shard_map/all_to_all | solution.py:183
  24.3 1.3 %broadcast_add_fusion = (s32[2]{0:T(128)}, s32[2]{0:T(128)S(1)}, s32[2]{0:T(128)}, s32[2]{0:T(128)S(1)}) fusion(s32[]{:T(128)S(6)} %sub.11, s32[2]{0:T(128)} %constant.76.clone, s32[]{:T(128)S(6)} %select_n.34, s32[2]{0:T(128)} %constant.77.clone), kind=kLoop, calls=%fused_computation.16 | loop fusion | flops 56 | bytes 56 | tf_op jit(solution)/shard_map/add | solution.py:209
  25.6 14.8 %all-to-all-done.states_ref = bf16[32,16,512]{2,1,0:T(8,128)(2,1)S(1)} async-done(((bf16[32,16,512]{2,1,0:T(8,128)(2,1)}), bf16[32,16,512]{2,1,0:T(8,128)(2,1)S(1)}, u32[]{:S(2)}, u32[]{:S(2)}) %all-to-all-start) | async-done | bytes 524320 | tf_op jit(solution)/shard_map/all_to_all | solution.py:183
  40.4 0.0 copy-start
  40.4 0.8 %copy-done = bf16[32,16,512]{2,1,0:T(8,128)(2,1)} copy-done((bf16[32,16,512]{2,1,0:T(8,128)(2,1)}, bf16[32,16,512]{2,1,0:T(8,128)(2,1)S(1)}, u32[]{:S(2)}) %copy-start) | copy-done | bytes 524312
  41.2 3.2 %shard_map.119.gated_ref = bf16[128,512]{1,0:T(8,128)(2,1)} custom-call(s32[1]{0:T(128)} %bitcast.ctx_ref, bf16[128,512]{1,0:T(8,128)(2,1)} %q_ref.1, bf16[128,512]{1,0:T(8,128)(2,1)} %k_ref.3, bf16[128,512]{1,0:T(8,128)(2,1)} %v_ref.3, bf16[8,512]{1,0:T(8,128)(2,1)} %copy-done.3, f32[3,3,512]{2,1,0:T(4,128)} %taps_ref.3, f32[16,512]{1,0:T(8,128)} %residue_ref.1, ...), custom_call_target="tpu_custom_call" | custom-call | tf_op jit(solution)/shard_map/pallas_call | solution.py:187
  44.4 3.3 %shard_map.122 = bf16[256,1024]{1,0:T(8,128)(2,1)} custom-call(s32[2]{0:T(128)} %get-tuple-element.9.order_ref, bf16[128,512]{1,0:T(8,128)(2,1)} %shard_map.119.gated_ref, bf16[512,8192]{1,0:T(8,128)(2,1)} %weight_ref.7), custom_call_target="tpu_custom_call" | custom-call | flops 268435456 | bytes 2621440 | tf_op jit(solution)/shard_map/pallas_call | solution.py:138
  47.7 0.0 collective-permute-start.2
  47.7 3.3 %shard_map.120 = bf16[256,1024]{1,0:T(8,128)(2,1)} custom-call(s32[2]{0:T(128)} %get-tuple-element.15.order_ref, bf16[128,512]{1,0:T(8,128)(2,1)} %shard_map.119.gated_ref, bf16[512,8192]{1,0:T(8,128)(2,1)} %weight_ref.7), custom_call_target="tpu_custom_call" | custom-call | flops 268435456 | bytes 2621440 | tf_op jit(solution)/shard_map/pallas_call | solution.py:138
  51.0 0.5 collective-permute-start.1
  51.5 0.6 broadcast_add_fusion.2.order_ref
  52.1 0.5 broadcast_add_fusion.3.order_ref
  52.6 0.0 collective-permute-done.2.other_ref
  52.6 0.0 copy-start.2
  52.6 0.8 %copy-done.2 = bf16[256,1024]{1,0:T(8,128)(2,1)} copy-done((bf16[256,1024]{1,0:T(8,128)(2,1)}, bf16[256,1024]{1,0:T(8,128)(2,1)S(1)}, u32[]{:S(2)}) %copy-start.2) | copy-done | bytes 524312
  53.4 3.4 %shard_map.123 = bf16[256,1024]{1,0:T(8,128)(2,1)} custom-call(s32[2]{0:T(128)} %broadcast_add_fusion.2.order_ref, bf16[128,512]{1,0:T(8,128)(2,1)} %shard_map.119.gated_ref, bf16[512,8192]{1,0:T(8,128)(2,1)} %weight_ref.7, bf16[256,1024]{1,0:T(8,128)(2,1)} %copy-done.2), custom_call_target="tpu_custom_call" | custom-call | flops 268435456 | bytes 2621440 | tf_op jit(solution)/shard_map/pallas_call | solution.py:138
  56.9 1.1 %fusion.9 = (bf16[128,1024]{1,0:T(8,128)(2,1)S(1)}, bf16[128,1024]{1,0:T(8,128)(2,1)S(1)}) fusion(bf16[256,1024]{1,0:T(8,128)(2,1)} %shard_map.123), kind=kLoop, calls=%fused_computation.20 | loop fusion | bytes 1048576 | tf_op jit(solution)/shard_map/slice | solution.py:218
  57.9 1.7 %collective-permute-start.3 = (bf16[128,1024]{1,0:T(8,128)(2,1)S(1)}, bf16[128,1024]{1,0:T(8,128)(2,1)S(1)}, u32[]{:S(2)}, u32[]{:S(2)}) collective-permute-start(bf16[128,1024]{1,0:T(8,128)(2,1)S(1)} %get-tuple-element.13), channel_id=1, source_target_pairs={{0,2},{1,3},{2,4},{3,5},{4,6},{5,7},{6,0},{7,1},{8,10},{9,11},{10,... | collective-permute-start | bytes 786440 | tf_op jit(solution)/shard_map/ppermute | solution.py:218
  59.6 2.9 %collective-permute-start.4 = (bf16[128,1024]{1,0:T(8,128)(2,1)S(1)}, bf16[128,1024]{1,0:T(8,128)(2,1)S(1)}, u32[]{:S(2)}, u32[]{:S(2)}) collective-permute-start(bf16[128,1024]{1,0:T(8,128)(2,1)S(1)} %get-tuple-element.14), channel_id=1, source_target_pairs={{0,4},{1,5},{2,6},{3,7},{4,0},{5,1},{6,2},{7,3},{8,12},{9,13},{10,... | collective-permute-start | bytes 786440 | tf_op jit(solution)/shard_map/ppermute | solution.py:217
  62.5 0.0 collective-permute-done.1.other_ref
  62.5 0.0 copy-start.1
  62.5 0.8 %copy-done.1 = bf16[256,1024]{1,0:T(8,128)(2,1)} copy-done((bf16[256,1024]{1,0:T(8,128)(2,1)}, bf16[256,1024]{1,0:T(8,128)(2,1)S(1)}, u32[]{:S(2)}) %copy-start.1) | copy-done | bytes 524312
  63.3 3.5 %shard_map.121 = f32[256,1024]{1,0:T(8,128)} custom-call(s32[2]{0:T(128)} %broadcast_add_fusion.3.order_ref, bf16[128,512]{1,0:T(8,128)(2,1)} %shard_map.119.gated_ref, bf16[512,8192]{1,0:T(8,128)(2,1)} %weight_ref.7, bf16[256,1024]{1,0:T(8,128)(2,1)} %copy-done.1), custom_call_target="tpu_custom_call" | custom-call | flops 268435456 | bytes 2621440 | tf_op jit(solution)/shard_map/pallas_call | solution.py:138
  66.8 1.1 %slice.42 = bf16[128,1024]{1,0:T(8,128)(2,1)S(1)} slice(f32[256,1024]{1,0:T(8,128)} %shard_map.121), slice={[0:128], [0:1024]} | slice | bytes 524288 | tf_op jit(solution)/shard_map/slice | solution.py:220
  67.9 1.4 %collective-permute-start.5 = (bf16[128,1024]{1,0:T(8,128)(2,1)S(1)}, bf16[128,1024]{1,0:T(8,128)(2,1)S(1)}, u32[]{:S(2)}, u32[]{:S(2)}) collective-permute-start(bf16[128,1024]{1,0:T(8,128)(2,1)S(1)} %slice.42), channel_id=1, source_target_pairs={{0,6},{1,7},{2,0},{3,1},{4,2},{5,3},{6,4},{7,5},{8,14},{9,15},{10,... | collective-permute-start | bytes 786440 | tf_op jit(solution)/shard_map/ppermute | solution.py:220
  69.3 0.0 collective-permute-done.3
  69.3 4.9 %collective-permute-done.4 = bf16[128,1024]{1,0:T(8,128)(2,1)S(1)} collective-permute-done((bf16[128,1024]{1,0:T(8,128)(2,1)S(1)}, bf16[128,1024]{1,0:T(8,128)(2,1)S(1)}, u32[]{:S(2)}, u32[]{:S(2)}) %collective-permute-start.4) | collective-permute-done | bytes 262176 | tf_op jit(solution)/shard_map/ppermute | solution.py:217
  74.3 1.4 %collective-permute-done.5 = bf16[128,1024]{1,0:T(8,128)(2,1)S(1)} collective-permute-done((bf16[128,1024]{1,0:T(8,128)(2,1)S(1)}, bf16[128,1024]{1,0:T(8,128)(2,1)S(1)}, u32[]{:S(2)}, u32[]{:S(2)}) %collective-permute-start.5) | collective-permute-done | bytes 262176 | tf_op jit(solution)/shard_map/ppermute | solution.py:220
  75.6 1.9 %fusion.2 = bf16[128,1024]{1,0:T(8,128)(2,1)} fusion(f32[256,1024]{1,0:T(8,128)} %shard_map.121, bf16[128,1024]{1,0:T(8,128)(2,1)S(1)} %collective-permute-done.5, bf16[128,1024]{1,0:T(8,128)(2,1)S(1)} %collective-permute-done.4, bf16[128,1024]{1,0:T(8,128)(2,1)S(1)} %collective-permute-done.3), kind=kLoop, calls=%fused_computation.4 | loop fusion | flops 917504 | bytes 1572864 | tf_op jit(solution)/shard_map/convert_element_type | solution.py:224
  (1 shorter events, 0.0 us)
Async XLA Ops:
  2.1 7.7 %collective-permute-start = (bf16[8,512]{1,0:T(8,128)(2,1)S(1)}, bf16[8,512]{1,0:T(8,128)(2,1)S(1)}, u32[]{:S(2)}, u32[]{:S(2)}) collective-permute-start(bf16[8,512]{1,0:T(8,128)(2,1)S(1)} %pad_maximum_fusion), channel_id=1, source_target_pairs={{0,8},{8,16},{16,24},{24,32},{32,40},{40,48},{48,56},{56,64},{64,7... | collective-permute-start | bytes 24584 | tf_op jit(solution)/shard_map/ppermute | solution.py:169
  9.8 0.6 copy-start.3
  14.3 26.1 %all-to-all-start = ((bf16[32,16,512]{2,1,0:T(8,128)(2,1)}), bf16[32,16,512]{2,1,0:T(8,128)(2,1)S(1)}, u32[]{:S(2)}, u32[]{:S(2)}) async-start(bf16[32,16,512]{2,1,0:T(8,128)(2,1)} %broadcast_in_dim.14), calls=%async_computation | async-start | bytes 1048576 | tf_op jit(solution)/shard_map/all_to_all | solution.py:183
  40.4 0.8 %copy-start = (bf16[32,16,512]{2,1,0:T(8,128)(2,1)}, bf16[32,16,512]{2,1,0:T(8,128)(2,1)S(1)}, u32[]{:S(2)}) copy-start(bf16[32,16,512]{2,1,0:T(8,128)(2,1)S(1)} %all-to-all-done.states_ref) | copy-start | bytes 1572868
  47.7 4.9 %collective-permute-start.2 = (bf16[256,1024]{1,0:T(8,128)(2,1)}, bf16[256,1024]{1,0:T(8,128)(2,1)S(1)}, u32[]{:S(2)}, u32[]{:S(2)}) collective-permute-start(bf16[256,1024]{1,0:T(8,128)(2,1)} %shard_map.122), channel_id=1, source_target_pairs={{0,1},{1,0},{2,3},{3,2},{4,5},{5,4},{6,7},{7,6},{8,9},{9,8},{10,11... | collective-permute-start | bytes 1572872 | tf_op jit(solution)/shard_map/ppermute | solution.py:213
  51.0 11.5 %collective-permute-start.1 = (bf16[256,1024]{1,0:T(8,128)(2,1)}, bf16[256,1024]{1,0:T(8,128)(2,1)S(1)}, u32[]{:S(2)}, u32[]{:S(2)}) collective-permute-start(bf16[256,1024]{1,0:T(8,128)(2,1)} %shard_map.120), channel_id=1, source_target_pairs={{0,1},{1,0},{2,3},{3,2},{4,5},{5,4},{6,7},{7,6},{8,9},{9,8},{10,11... | collective-permute-start | bytes 1572872 | tf_op jit(solution)/shard_map/ppermute | solution.py:215
  52.6 0.8 %copy-start.2 = (bf16[256,1024]{1,0:T(8,128)(2,1)}, bf16[256,1024]{1,0:T(8,128)(2,1)S(1)}, u32[]{:S(2)}) copy-start(bf16[256,1024]{1,0:T(8,128)(2,1)S(1)} %collective-permute-done.2.other_ref) | copy-start | bytes 1572868
  57.9 11.4 %collective-permute-start.3 = (bf16[128,1024]{1,0:T(8,128)(2,1)S(1)}, bf16[128,1024]{1,0:T(8,128)(2,1)S(1)}, u32[]{:S(2)}, u32[]{:S(2)}) collective-permute-start(bf16[128,1024]{1,0:T(8,128)(2,1)S(1)} %get-tuple-element.13), channel_id=1, source_target_pairs={{0,2},{1,3},{2,4},{3,5},{4,6},{5,7},{6,0},{7,1},{8,10},{9,11},{10,... | collective-permute-start | bytes 786440 | tf_op jit(solution)/shard_map/ppermute | solution.py:218
  59.6 14.7 %collective-permute-start.4 = (bf16[128,1024]{1,0:T(8,128)(2,1)S(1)}, bf16[128,1024]{1,0:T(8,128)(2,1)S(1)}, u32[]{:S(2)}, u32[]{:S(2)}) collective-permute-start(bf16[128,1024]{1,0:T(8,128)(2,1)S(1)} %get-tuple-element.14), channel_id=1, source_target_pairs={{0,4},{1,5},{2,6},{3,7},{4,0},{5,1},{6,2},{7,3},{8,12},{9,13},{10,... | collective-permute-start | bytes 786440 | tf_op jit(solution)/shard_map/ppermute | solution.py:217
  62.5 0.8 %copy-start.1 = (bf16[256,1024]{1,0:T(8,128)(2,1)}, bf16[256,1024]{1,0:T(8,128)(2,1)S(1)}, u32[]{:S(2)}) copy-start(bf16[256,1024]{1,0:T(8,128)(2,1)S(1)} %collective-permute-done.1.other_ref) | copy-start | bytes 1572868
  67.9 7.7 %collective-permute-start.5 = (bf16[128,1024]{1,0:T(8,128)(2,1)S(1)}, bf16[128,1024]{1,0:T(8,128)(2,1)S(1)}, u32[]{:S(2)}, u32[]{:S(2)}) collective-permute-start(bf16[128,1024]{1,0:T(8,128)(2,1)S(1)} %slice.42), channel_id=1, source_target_pairs={{0,6},{1,7},{2,0},{3,1},{4,2},{5,3},{6,4},{7,5},{8,14},{9,15},{10,... | collective-permute-start | bytes 786440 | tf_op jit(solution)/shard_map/ppermute | solution.py:220

commit v2 on v1

--- a/solution.py
+++ b/solution.py
@@ -111,45 +111,56 @@
         gated_ref[:, cols] = (query[:, at : at + LANES] * long).astype(gated_ref.dtype)
 
 
-def project_kernel(order_ref, gated_ref, weight_ref, out_ref):
-    out_ref[...] = jnp.dot(gated_ref[...], weight_ref[...], preferred_element_type=F32).astype(
-        out_ref.dtype
-    )
-
-
-def project_add_kernel(order_ref, gated_ref, weight_ref, other_ref, out_ref):
-    out_ref[...] = (
-        jnp.dot(gated_ref[...], weight_ref[...], preferred_element_type=F32)
-        + other_ref[...].astype(F32)
-    ).astype(out_ref.dtype)
-
-
-def project(order, gated, weight, width, other=None, dtype=BF16):
-    rows, depth = gated.shape
-    count = order.shape[0]
-    specs = [
-        pl.BlockSpec((rows, depth), lambda i, o: (0, 0)),
-        pl.BlockSpec((depth, width), lambda i, o: (0, o[i])),
-    ]
-    operands = [order, gated, weight]
-    if other is not None:
-        specs.append(pl.BlockSpec((rows, width), lambda i, o: (i, 0)))
-        operands.append(other)
-    return pl.pallas_call(
-        project_kernel if other is None else project_add_kernel,
-        out_shape=jax.ShapeDtypeStruct((count * rows, width), dtype),
-        grid_spec=pltpu.PrefetchScalarGridSpec(
-            num_scalar_prefetch=1,
-            grid=(count,),
-            in_specs=specs,
-            out_specs=pl.BlockSpec((rows, width), lambda i, o: (i, 0)),
-        ),
-        cost_estimate=pl.CostEstimate(
-            flops=2 * rows * depth * width * count,
-            bytes_accessed=2 * count * width * (depth + rows),
-            transcendentals=0,
-        ),
-    )(*operands)
+def start_weights(order_ref, weight_ref, held, arrived):
+    chunk = held.shape[2]
+    copies = []
+    for i in range(held.shape[0]):
+        columns = pl.ds(pl.multiple_of(order_ref[i] * chunk, chunk), chunk)
+        copy = pltpu.make_async_copy(weight_ref.at[:, columns], held.at[i], arrived.at[i])
+        copy.start()
+        copies.append(copy)
+    return copies
+
+
+def project_chunks(copies, gated, held, outs):
+    for i, copy in enumerate(copies):
+        copy.wait()
+        each = len(copies) // len(outs)
+        out = outs[i // each]
+        out[i % each] = jnp.dot(gated, held[i], preferred_element_type=F32).astype(out.dtype)
+
+
+def gate_project_kernel(ctx_ref, order_ref, *refs):
+    *inputs, weight_ref, gated_ref, first_ref, second_ref = refs[:14]
+    mixed, carry, convolved, held, arrived = refs[14:]
+    copies = start_weights(order_ref, weight_ref, held, arrived)
+    gate_kernel(ctx_ref, *inputs, gated_ref, mixed, carry, convolved)
+    project_chunks(copies, gated_ref[...], held, (first_ref, second_ref))
+
+
+def project_kernel(order_ref, gated_ref, weight_ref, first_ref, second_ref, held, arrived):
+    copies = start_weights(order_ref, weight_ref, held, arrived)
+    project_chunks(copies, gated_ref[...], held, (first_ref, second_ref))
+
+
+def first_sums_kernel(kept_ref, swapped_ref, to_a_ref, to_b_ref):
+    for i in range(2):
+        for out, at in ((to_a_ref, i), (to_b_ref, 2 + i)):
+            out[i] = (kept_ref[at] + swapped_ref[at].astype(F32)).astype(out.dtype)
+
+
+def second_sums_kernel(kept_ref, swapped_ref, from_ref, sum_ref, *, at):
+    total = kept_ref[at] + swapped_ref[at].astype(F32) + from_ref[1].astype(F32)
+    sum_ref[...] = total.astype(sum_ref.dtype)
+
+
+def last_sums_kernel(kept_ref, swapped_ref, from_a_ref, from_b_ref, last_b_ref, last_a_ref, out_ref):
+    chunk = kept_ref.shape[2]
+    for half, (near, last) in enumerate(((from_a_ref, last_b_ref), (from_b_ref, last_a_ref))):
+        at = 2 * half + 1
+        total = kept_ref[at] + swapped_ref[at].astype(F32)
+        total = total + near[0].astype(F32) + last[...].astype(F32)
+        out_ref[:, half * chunk : (half + 1) * chunk] = total.astype(out_ref.dtype)
 
 
 def body(
@@ -184,44 +195,74 @@
         jnp.broadcast_to(state[None], (blocks, modes, width)), "ctx", 0, 0
     )
 
-    gated = pl.pallas_call(
-        gate_kernel,
-        out_shape=jax.ShapeDtypeStruct((rows, width), BF16),
-        in_specs=[pl.BlockSpec(memory_space=pltpu.SMEM)] + [whole] * 10,
-        out_specs=whole,
+    partner_core = [(i, i ^ 1) for i in range(parts)]
+    pairing_a = [(i, (i // 2 ^ 1) * 2 + i % 2) for i in range(parts)]
+    pairing_b = [(i, (chips - 1 - i // 2) * 2 + i % 2) for i in range(parts)]
+    chip, core = ch // 2, ch % 2
+    chip_a, chip_b, chip_c = chip ^ 1, chips - 1 - chip, (chips - 1 - chip) ^ 1
+    chunk = out_weight.shape[1] // parts // 2
+
+    def chunks_of(core):
+        base = jnp.stack([chip_a, chip_c, chip_b, chip_c, chip_b, chip, chip_a, chip])
+        half = jnp.array([0, 0, 1, 1, 0, 0, 1, 1], jnp.int32)
+        return (base.astype(jnp.int32) * 2 + core) * 2 + half
+
+    smem = pl.BlockSpec(memory_space=pltpu.SMEM)
+    hbm = pl.BlockSpec(memory_space=pl.ANY)
+    weights = [pltpu.VMEM((8, width, chunk), BF16), pltpu.SemaphoreType.DMA((8,))]
+
+    def chunks_like(dtype):
+        return jax.ShapeDtypeStruct((4, rows, chunk), dtype)
+
+    gated, sent1, sent2 = pl.pallas_call(
+        gate_project_kernel,
+        out_shape=(jax.ShapeDtypeStruct((rows, width), BF16), chunks_like(BF16), chunks_like(BF16)),
+        in_specs=[smem] * 2 + [whole] * 10 + [hbm],
+        out_specs=(whole,) * 3,
         scratch_shapes=[
             pltpu.VMEM((width // LANES, rows, LANES), F32),
             pltpu.VMEM((modes, width), F32),
             pltpu.VMEM((width // LANES, rows, LANES), F32),
-        ],
+        ] + weights,
     )(
-        ctx[None].astype(jnp.int32), query_input, key_input, value_input, halo, short_weight,
-        residue, decay_rate, skip_gain[None], states, ends,
-    )
-
-    columns = out_weight.shape[1] // parts
-    core_swap = [(i, i ^ 1) for i in range(parts)]
-
-    def along_y(apart):
-        return [(i, (i + 2 * apart) % parts) for i in range(parts)]
-
-    def blocks_for(offsets, core):
-        return (ch // 2 + jnp.array(offsets, jnp.int32)) % chips * 2 + core
-
-    mine, partner = ch % 2, 1 - ch % 2
-    sent_a = project(blocks_for((2, 1), partner), gated, out_weight, columns)
-    got_a = lax.ppermute(sent_a, "ch", core_swap)
-    sent_b = project(blocks_for((3, 0), partner), gated, out_weight, columns)
-    got_b = lax.ppermute(sent_b, "ch", core_swap)
-    far = project(blocks_for((2, 1), mine), gated, out_weight, columns, got_a)
-    from2 = lax.ppermute(far[:rows], "ch", along_y(2))
-    from1 = lax.ppermute(far[rows:], "ch", along_y(1))
-    near = project(blocks_for((3, 0), mine), gated, out_weight, columns, got_b, F32)
-    from3 = lax.ppermute(near[:rows].astype(BF16), "ch", along_y(3))
-    total = (
-        near[rows:] + from1.astype(F32) + from2.astype(F32) + from3.astype(F32)
-    )
-    return total.astype(BF16)
+        ctx[None].astype(jnp.int32), chunks_of(1 - core), query_input, key_input, value_input,
+        halo, short_weight, residue, decay_rate, skip_gain[None], states, ends, out_weight,
+    )
+    got1 = lax.ppermute(sent1, "ch", partner_core)
+    got2 = lax.ppermute(sent2, "ch", partner_core)
+    kept1, kept2 = pl.pallas_call(
+        project_kernel,
+        out_shape=(chunks_like(F32), chunks_like(F32)),
+        in_specs=[smem, whole, hbm],
+        out_specs=(whole,) * 2,
+        scratch_shapes=weights,
+        cost_estimate=pl.CostEstimate(
+            flops=2 * rows * width * chunk * 8, bytes_accessed=16 * width * chunk, transcendentals=0
+        ),
+    )(chunks_of(core), gated, out_weight)
+    half_pair = jax.ShapeDtypeStruct((2, rows, chunk), BF16)
+    to_a, to_b = pl.pallas_call(
+        first_sums_kernel, out_shape=(half_pair,) * 2, in_specs=[whole] * 2, out_specs=(whole,) * 2
+    )(kept1, got1)
+    from_a = lax.ppermute(to_a, "ch", pairing_a)
+    from_b = lax.ppermute(to_b, "ch", pairing_b)
+
+    def second_sum(near, at):
+        return pl.pallas_call(
+            functools.partial(second_sums_kernel, at=at),
+            out_shape=jax.ShapeDtypeStruct((rows, chunk), BF16),
+            in_specs=[whole] * 3,
+            out_specs=whole,
+        )(kept2, got2, near)
+
+    last_b = lax.ppermute(second_sum(from_a, 0), "ch", pairing_b)
+    last_a = lax.ppermute(second_sum(from_b, 2), "ch", pairing_a)
+    return pl.pallas_call(
+        last_sums_kernel,
+        out_shape=jax.ShapeDtypeStruct((rows, 2 * chunk), BF16),
+        in_specs=[whole] * 6,
+        out_specs=whole,
+    )(kept2, got2, from_a, from_b, last_b, last_a)
 
 
 def solution(mesh):

time: 78.5 us -> 81.2 us (1.034)
  waiting for transfers between devices: 25.4 us -> 28.9 us
  other arithmetic: 4.28 us -> 1.22 us
  Pallas kernels: 19.2 us -> 21.6 us
  starting transfers between devices: 19.8 us -> 20.8 us
  local copies, waits for them, and re-layouts: 8.82 us -> 8 us
    ppermute x5 -> x6, waiting for transfers between devices: 6.31 us -> 9.8 us  [the longest x1 4.75 us: body(): from_a = lax.ppermute(to_a, 'ch', pairing_a)]
    pallas_call x5 -> x6, Pallas kernels: 16.8 us -> 19.2 us  [the longest x1 5.38 us: body(): pl.pallas_call(gate_project_kernel, out_shape=(jax.ShapeDtypeStruct((rows...]
    slice x2 -> x0, local copies, waits for them, and re-layouts: 2.13 us -> none  [the longest x1 1.07 us: body(): from3 = lax.ppermute(near[:rows].astype(BF16), 'ch', along_y(3))]
    convert_element_type x1 -> x0, other arithmetic: 1.89 us -> none  [body(): return total.astype(BF16)]
    unnamed x8 -> x16, local copies, waits for them, and re-layouts: 3.02 us -> 4.23 us
    add x3 -> x1, other arithmetic: 2.38 us -> 1.2 us  [chunks_of(): return (base.astype(jnp.int32) * 2 + core) * 2 + half]
    ppermute x5 -> x6, starting transfers between devices: 6.49 us -> 7.5 us  [the longest x1 3.02 us: body(): last_b = lax.ppermute(second_sum(from_a, 0), 'ch', pairing_b)]
  transfers between devices with their start and end apart: 7 -> 8, of which waited for: 4 -> 5; matrix products, arithmetic and copies ran while one was open for 6% -> 2% of each run, Pallas kernels for 13% -> 14%
where the time goes in v2:
time: 81.2 us; the launch traced here: 80.6 us
  waiting for transfers between devices  28.9 us (36%)
  Pallas kernels  21.6 us (27%)
  starting transfers between devices  20.8 us (26%)
  local copies, waits for them, and re-layouts  8 us (10%)
  other arithmetic  1.22 us (2%)
    all_to_all x1, waiting for transfers between devices, body(): lax.all_to_all(jnp.broadcast_to(state[None], (blocks, modes, width)), 'ct...  14.8 us
    all_to_all x1, starting transfers between devices, body(): lax.all_to_all(jnp.broadcast_to(state[None], (blocks, modes, width)), 'ct...  9.94 us
    pallas_call x1, Pallas kernels, body(): pl.pallas_call(gate_project_kernel, out_shape=(jax.ShapeDtypeStruct((rows...  5.38 us
    pallas_call x1, Pallas kernels, body(): pl.pallas_call(project_kernel, out_shape=(chunks_like(F32), chunks_like(F...  5.01 us
    ppermute x1, waiting for transfers between devices, body(): from_a = lax.ppermute(to_a, 'ch', pairing_a)  4.75 us
    ppermute x1, waiting for transfers between devices, body(): last_a = lax.ppermute(second_sum(from_b, 2), 'ch', pairing_a)  4.62 us
    ppermute x1, waiting for transfers between devices, body(): halo = lax.ppermute(edge, 'ctx', [(i, i + 1) for i in range(blocks - 1)])  4.25 us
    unnamed x16, local copies, waits for them, and re-layouts  4.23 us
  transfers between devices with their start and end apart: 8, of which 5 were waited for; matrix products, arithmetic and copies ran while one was open for 2% of the time, Pallas kernels for 14%

profile of v2, /device:TPU:32, one launch (start us, length us, event | category | flops | bytes accessed | tf_op | source)
XLA Modules:
  0.0 80.6 jit_solution(16015977244590689707)
XLA Ops:
  0.0 0.7 slice.12
  0.7 0.7 slice.10
  1.4 0.7 slice.11
  2.1 3.4 %collective-permute-start = (bf16[8,512]{1,0:T(8,128)(2,1)S(1)}, bf16[8,512]{1,0:T(8,128)(2,1)S(1)}, u32[]{:S(2)}, u32[]{:S(2)}) collective-permute-start(bf16[8,512]{1,0:T(8,128)(2,1)S(1)} %pad_maximum_fusion), channel_id=1, source_target_pairs={{0,8},{8,16},{16,24},{24,32},{32,40},{40,48},{48,56},{56,64},{64,7... | collective-permute-start | bytes 24584 | tf_op jit(solution)/shard_map/ppermute | solution.py:180
  5.5 4.2 %collective-permute-done.halo_ref.refs_3_ = bf16[8,512]{1,0:T(8,128)(2,1)S(1)} collective-permute-done((bf16[8,512]{1,0:T(8,128)(2,1)S(1)}, bf16[8,512]{1,0:T(8,128)(2,1)S(1)}, u32[]{:S(2)}, u32[]{:S(2)}) %collective-permute-start) | collective-permute-done | bytes 8224 | tf_op jit(solution)/shard_map/ppermute | solution.py:180
  9.8 0.0 copy-start.7
  9.8 0.6 copy-done.7
  10.4 2.4 %shard_map.100 = (bf16[16,512]{1,0:T(8,128)(2,1)}, f32[16,8,512]{2,1,0:T(8,128)}) custom-call(bf16[128,512]{1,0:T(8,128)(2,1)} %refs_1_.1, bf16[128,512]{1,0:T(8,128)(2,1)} %refs_2_.1, bf16[8,512]{1,0:T(8,128)(2,1)} %copy-done.7, f32[3,3,512]{2,1,0:T(4,128)} %refs_4_.1, f32[16,512]{1,0:T(8,128)} %refs_6_.1), custom_call_target="tpu_custom_call" | custom-call | tf_op jit(solution)/shard_map/pallas_call | solution.py:183
  12.7 1.6 %broadcast_in_dim.14 = bf16[32,16,512]{2,1,0:T(8,128)(2,1)} broadcast(bf16[16,512]{1,0:T(8,128)(2,1)} %get-tuple-element.14), dimensions={1,2} | broadcast | bytes 540672 | tf_op jit(solution)/shard_map/broadcast_in_dim | solution.py:195
  14.3 9.9 %all-to-all-start = ((bf16[32,16,512]{2,1,0:T(8,128)(2,1)}), bf16[32,16,512]{2,1,0:T(8,128)(2,1)S(1)}, u32[]{:S(2)}, u32[]{:S(2)}) async-start(bf16[32,16,512]{2,1,0:T(8,128)(2,1)} %broadcast_in_dim.14), calls=%async_computation | async-start | bytes 1048576 | tf_op jit(solution)/shard_map/all_to_all | solution.py:194
  24.3 0.1 stack.14
  24.4 1.2 %multiply_add_fusion = (s32[8]{0:T(128)}, s32[8]{0:T(128)}) fusion(s32[8]{0:T(128)} %constant.39.clone, s32[8]{0:T(128)S(1)} %stack.14, s32[]{:T(128)S(6)} %sub.13, s32[]{:T(128)S(6)} %select_n.12), kind=kLoop, calls=%fused_computation.1 | loop fusion | flops 56 | bytes 136 | tf_op jit(solution)/shard_map/add | solution.py:208
  25.6 14.8 %all-to-all-done.refs_8_ = bf16[32,16,512]{2,1,0:T(8,128)(2,1)S(1)} async-done(((bf16[32,16,512]{2,1,0:T(8,128)(2,1)}), bf16[32,16,512]{2,1,0:T(8,128)(2,1)S(1)}, u32[]{:S(2)}, u32[]{:S(2)}) %all-to-all-start) | async-done | bytes 524320 | tf_op jit(solution)/shard_map/all_to_all | solution.py:194
  40.4 0.0 copy-start.1
  40.4 0.8 copy-done.1
  41.2 5.4 %shard_map.101 = (bf16[128,512]{1,0:T(8,128)(2,1)}, bf16[4,128,512]{2,1,0:T(8,128)(2,1)}, bf16[4,128,512]{2,1,0:T(8,128)(2,1)}) custom-call(s32[1]{0:T(128)} %bitcast.4.ctx_ref, s32[8]{0:T(128)} %get-tuple-element.23.order_ref, bf16[128,512]{1,0:T(8,128)(2,1)} %refs_0_.1, bf16[128,512]{1,0:T(8,128)(2,1)} %refs_1_.1, bf16[128,512]{1,0:T(8,128)(2,1)} %refs_2_.1, ...), custom_call_target="tpu_custom_call" | custom-call | tf_op jit(solution)/shard_map/pallas_call | solution.py:217
  46.6 0.1 collective-permute-start.2
  46.7 0.5 collective-permute-start.1
  47.2 5.0 %shard_map.102 = (f32[4,128,512]{2,1,0:T(8,128)}, f32[4,128,512]{2,1,0:T(8,128)}) custom-call(s32[8]{0:T(128)} %get-tuple-element.24.order_ref, bf16[128,512]{1,0:T(8,128)(2,1)} %get-tuple-element.16.gated_ref, bf16[512,8192]{1,0:T(8,128)(2,1)} %weight_ref.1), custom_call_target="tpu_custom_call" | custom-call | flops 536870912 | bytes 4194304 | tf_op jit(solution)/shard_map/pallas_call | solution.py:233
  52.2 0.0 collective-permute-done.2.swapped_ref
  52.2 0.0 copy-start.4
  52.2 0.8 copy-done.4
  53.0 2.2 %shard_map.103 = (bf16[2,128,512]{2,1,0:T(8,128)(2,1)}, bf16[2,128,512]{2,1,0:T(8,128)(2,1)}) custom-call(f32[4,128,512]{2,1,0:T(8,128)} %get-tuple-element.19.kept_ref, bf16[4,128,512]{2,1,0:T(8,128)(2,1)} %copy-done.4), custom_call_target="tpu_custom_call" | custom-call | tf_op jit(solution)/shard_map/pallas_call | solution.py:244
  55.2 1.6 %collective-permute-start.3 = (bf16[2,128,512]{2,1,0:T(8,128)(2,1)}, bf16[2,128,512]{2,1,0:T(8,128)(2,1)S(1)}, u32[]{:S(2)}, u32[]{:S(2)}) collective-permute-start(bf16[2,128,512]{2,1,0:T(8,128)(2,1)} %get-tuple-element.21), channel_id=1, source_target_pairs={{0,2},{1,3},{2,0},{3,1},{4,6},{5,7},{6,4},{7,5},{8,10},{9,11},{10,... | collective-permute-start | bytes 786440 | tf_op jit(solution)/shard_map/ppermute | solution.py:247
  56.8 2.2 %collective-permute-start.4 = (bf16[2,128,512]{2,1,0:T(8,128)(2,1)}, bf16[2,128,512]{2,1,0:T(8,128)(2,1)S(1)}, u32[]{:S(2)}, u32[]{:S(2)}) collective-permute-start(bf16[2,128,512]{2,1,0:T(8,128)(2,1)} %get-tuple-element.22), channel_id=1, source_target_pairs={{0,6},{1,7},{2,4},{3,5},{4,2},{5,3},{6,0},{7,1},{8,14},{9,15},{10,... | collective-permute-start | bytes 786440 | tf_op jit(solution)/shard_map/ppermute | solution.py:248
  59.0 0.0 collective-permute-done.1.swapped_ref
  59.0 0.0 copy-start
  59.0 4.8 %collective-permute-done.3.from_ref.from_a_ref = bf16[2,128,512]{2,1,0:T(8,128)(2,1)S(1)} collective-permute-done((bf16[2,128,512]{2,1,0:T(8,128)(2,1)}, bf16[2,128,512]{2,1,0:T(8,128)(2,1)S(1)}, u32[]{:S(2)}, u32[]{:S(2)}) %collective-permute-start.3) | collective-permute-done | bytes 262176 | tf_op jit(solution)/shard_map/ppermute | solution.py:247
  63.7 0.0 copy-start.2
  63.7 0.0 copy-done
  63.8 0.7 copy-done.2
  64.4 2.1 %shard_map.104 = bf16[128,512]{1,0:T(8,128)(2,1)} custom-call(f32[4,128,512]{2,1,0:T(8,128)} %get-tuple-element.17.kept_ref, bf16[4,128,512]{2,1,0:T(8,128)(2,1)} %copy-done, bf16[2,128,512]{2,1,0:T(8,128)(2,1)} %copy-done.2), custom_call_target="tpu_custom_call" | custom-call | tf_op jit(solution)/shard_map/pallas_call | solution.py:251
  66.6 3.0 %collective-permute-start.5 = (bf16[128,512]{1,0:T(8,128)(2,1)}, bf16[128,512]{1,0:T(8,128)(2,1)S(1)}, u32[]{:S(2)}, u32[]{:S(2)}) collective-permute-start(bf16[128,512]{1,0:T(8,128)(2,1)} %shard_map.104), channel_id=1, source_target_pairs={{0,6},{1,7},{2,4},{3,5},{4,2},{5,3},{6,0},{7,1},{8,14},{9,15},{10,... | collective-permute-start | bytes 393224 | tf_op jit(solution)/shard_map/ppermute | solution.py:258
  69.6 0.0 collective-permute-done.4.from_ref.from_b_ref
  69.6 0.0 copy-start.3
  69.6 0.7 copy-done.3
  70.3 2.1 %shard_map.105 = bf16[128,512]{1,0:T(8,128)(2,1)} custom-call(f32[4,128,512]{2,1,0:T(8,128)} %get-tuple-element.17.kept_ref, bf16[4,128,512]{2,1,0:T(8,128)(2,1)} %copy-done, bf16[2,128,512]{2,1,0:T(8,128)(2,1)} %copy-done.3), custom_call_target="tpu_custom_call" | custom-call | tf_op jit(solution)/shard_map/pallas_call | solution.py:251
  72.4 0.1 collective-permute-start.6
  72.5 0.4 collective-permute-done.5.last_b_ref
  72.9 0.0 copy-start.5
  72.9 4.6 %collective-permute-done.6.last_a_ref = bf16[128,512]{1,0:T(8,128)(2,1)S(1)} collective-permute-done((bf16[128,512]{1,0:T(8,128)(2,1)}, bf16[128,512]{1,0:T(8,128)(2,1)S(1)}, u32[]{:S(2)}, u32[]{:S(2)}) %collective-permute-start.6) | collective-permute-done | bytes 131104 | tf_op jit(solution)/shard_map/ppermute | solution.py:259
  77.6 0.0 copy-done.5
  77.6 0.0 copy-start.6
  77.6 0.6 copy-done.6
  78.2 2.4 %shard_map.106 = bf16[128,1024]{1,0:T(8,128)(2,1)} custom-call(f32[4,128,512]{2,1,0:T(8,128)} %get-tuple-element.17.kept_ref, bf16[4,128,512]{2,1,0:T(8,128)(2,1)} %copy-done, bf16[2,128,512]{2,1,0:T(8,128)(2,1)} %copy-done.2, bf16[2,128,512]{2,1,0:T(8,128)(2,1)} %copy-done.3, bf16[128,512]{1,0:T(8,128)(2,1)} %copy-done.5, bf16[128,512]{1,0:T(8,128)(2,1)} %copy-done.6), custom_call_target="tpu_custom_call" | custom-call | tf_op jit(solution)/shard_map/pallas_call | solution.py:260
  (1 shorter events, 0.0 us)
Async XLA Ops:
  2.1 7.7 %collective-permute-start = (bf16[8,512]{1,0:T(8,128)(2,1)S(1)}, bf16[8,512]{1,0:T(8,128)(2,1)S(1)}, u32[]{:S(2)}, u32[]{:S(2)}) collective-permute-start(bf16[8,512]{1,0:T(8,128)(2,1)S(1)} %pad_maximum_fusion), channel_id=1, source_target_pairs={{0,8},{8,16},{16,24},{24,32},{32,40},{40,48},{48,56},{56,64},{64,7... | collective-permute-start | bytes 24584 | tf_op jit(solution)/shard_map/ppermute | solution.py:180
  9.8 0.6 copy-start.7
  14.3 26.1 %all-to-all-start = ((bf16[32,16,512]{2,1,0:T(8,128)(2,1)}), bf16[32,16,512]{2,1,0:T(8,128)(2,1)S(1)}, u32[]{:S(2)}, u32[]{:S(2)}) async-start(bf16[32,16,512]{2,1,0:T(8,128)(2,1)} %broadcast_in_dim.14), calls=%async_computation | async-start | bytes 1048576 | tf_op jit(solution)/shard_map/all_to_all | solution.py:194
  40.4 0.8 copy-start.1
  46.6 5.6 %collective-permute-start.2 = (bf16[4,128,512]{2,1,0:T(8,128)(2,1)}, bf16[4,128,512]{2,1,0:T(8,128)(2,1)S(1)}, u32[]{:S(2)}, u32[]{:S(2)}) collective-permute-start(bf16[4,128,512]{2,1,0:T(8,128)(2,1)} %get-tuple-element.20), channel_id=1, source_target_pairs={{0,1},{1,0},{2,3},{3,2},{4,5},{5,4},{6,7},{7,6},{8,9},{9,8},{10,11... | collective-permute-start | bytes 1572872 | tf_op jit(solution)/shard_map/ppermute | solution.py:231
  46.7 12.3 %collective-permute-start.1 = (bf16[4,128,512]{2,1,0:T(8,128)(2,1)}, bf16[4,128,512]{2,1,0:T(8,128)(2,1)S(1)}, u32[]{:S(2)}, u32[]{:S(2)}) collective-permute-start(bf16[4,128,512]{2,1,0:T(8,128)(2,1)} %get-tuple-element.18), channel_id=1, source_target_pairs={{0,1},{1,0},{2,3},{3,2},{4,5},{5,4},{6,7},{7,6},{8,9},{9,8},{10,11... | collective-permute-start | bytes 1572872 | tf_op jit(solution)/shard_map/ppermute | solution.py:232
  52.2 0.8 copy-start.4
  55.2 8.5 %collective-permute-start.3 = (bf16[2,128,512]{2,1,0:T(8,128)(2,1)}, bf16[2,128,512]{2,1,0:T(8,128)(2,1)S(1)}, u32[]{:S(2)}, u32[]{:S(2)}) collective-permute-start(bf16[2,128,512]{2,1,0:T(8,128)(2,1)} %get-tuple-element.21), channel_id=1, source_target_pairs={{0,2},{1,3},{2,0},{3,1},{4,6},{5,7},{6,4},{7,5},{8,10},{9,11},{10,... | collective-permute-start | bytes 786440 | tf_op jit(solution)/shard_map/ppermute | solution.py:247
  56.8 12.8 %collective-permute-start.4 = (bf16[2,128,512]{2,1,0:T(8,128)(2,1)}, bf16[2,128,512]{2,1,0:T(8,128)(2,1)S(1)}, u32[]{:S(2)}, u32[]{:S(2)}) collective-permute-start(bf16[2,128,512]{2,1,0:T(8,128)(2,1)} %get-tuple-element.22), channel_id=1, source_target_pairs={{0,6},{1,7},{2,4},{3,5},{4,2},{5,3},{6,0},{7,1},{8,14},{9,15},{10,... | collective-permute-start | bytes 786440 | tf_op jit(solution)/shard_map/ppermute | solution.py:248
  59.0 4.8 %copy-start = (bf16[4,128,512]{2,1,0:T(8,128)(2,1)}, bf16[4,128,512]{2,1,0:T(8,128)(2,1)S(1)}, u32[]{:S(2)}) copy-start(bf16[4,128,512]{2,1,0:T(8,128)(2,1)S(1)} %collective-permute-done.1.swapped_ref) | copy-start | bytes 1572868
  63.7 0.7 copy-start.2
  66.6 6.4 %collective-permute-start.5 = (bf16[128,512]{1,0:T(8,128)(2,1)}, bf16[128,512]{1,0:T(8,128)(2,1)S(1)}, u32[]{:S(2)}, u32[]{:S(2)}) collective-permute-start(bf16[128,512]{1,0:T(8,128)(2,1)} %shard_map.104), channel_id=1, source_target_pairs={{0,6},{1,7},{2,4},{3,5},{4,2},{5,3},{6,0},{7,1},{8,14},{9,15},{10,... | collective-permute-start | bytes 393224 | tf_op jit(solution)/shard_map/ppermute | solution.py:258
  69.6 0.7 copy-start.3
  72.4 5.2 %collective-permute-start.6 = (bf16[128,512]{1,0:T(8,128)(2,1)}, bf16[128,512]{1,0:T(8,128)(2,1)S(1)}, u32[]{:S(2)}, u32[]{:S(2)}) collective-permute-start(bf16[128,512]{1,0:T(8,128)(2,1)} %shard_map.105), channel_id=1, source_target_pairs={{0,2},{1,3},{2,0},{3,1},{4,6},{5,7},{6,4},{7,5},{8,10},{9,11},{10,... | collective-permute-start | bytes 393224 | tf_op jit(solution)/shard_map/ppermute | solution.py:259
  72.9 4.6 %copy-start.5 = (bf16[128,512]{1,0:T(8,128)(2,1)}, bf16[128,512]{1,0:T(8,128)(2,1)S(1)}, u32[]{:S(2)}) copy-start(bf16[128,512]{1,0:T(8,128)(2,1)S(1)} %collective-permute-done.5.last_b_ref) | copy-start | bytes 393220
  77.6 0.6 copy-start.6

commit v3 on v2

--- a/solution.py
+++ b/solution.py
@@ -11,6 +11,8 @@
 BF16 = jnp.bfloat16
 SUBLANES = 8
 LANES = 128
+ROOM = pltpu.CompilerParams(vmem_limit_bytes=16 * 2**20)
+SOME_ROOM = pltpu.CompilerParams(vmem_limit_bytes=50 * 2**20)
 
 
 def rows_of(shape):
@@ -232,6 +234,7 @@
     got2 = lax.ppermute(sent2, "ch", partner_core)
     kept1, kept2 = pl.pallas_call(
         project_kernel,
+        compiler_params=SOME_ROOM,
         out_shape=(chunks_like(F32), chunks_like(F32)),
         in_specs=[smem, whole, hbm],
         out_specs=(whole,) * 2,
@@ -242,7 +245,7 @@
     )(chunks_of(core), gated, out_weight)
     half_pair = jax.ShapeDtypeStruct((2, rows, chunk), BF16)
     to_a, to_b = pl.pallas_call(
-        first_sums_kernel, out_shape=(half_pair,) * 2, in_specs=[whole] * 2, out_specs=(whole,) * 2
+        first_sums_kernel, compiler_params=ROOM, out_shape=(half_pair,) * 2, in_specs=[whole] * 2, out_specs=(whole,) * 2
     )(kept1, got1)
     from_a = lax.ppermute(to_a, "ch", pairing_a)
     from_b = lax.ppermute(to_b, "ch", pairing_b)
@@ -250,6 +253,7 @@
     def second_sum(near, at):
         return pl.pallas_call(
             functools.partial(second_sums_kernel, at=at),
+            compiler_params=ROOM,
             out_shape=jax.ShapeDtypeStruct((rows, chunk), BF16),
             in_specs=[whole] * 3,
             out_specs=whole,
@@ -259,6 +263,7 @@
     last_a = lax.ppermute(second_sum(from_b, 2), "ch", pairing_a)
     return pl.pallas_call(
         last_sums_kernel,
+        compiler_params=ROOM,
         out_shape=jax.ShapeDtypeStruct((rows, 2 * chunk), BF16),
         in_specs=[whole] * 6,
         out_specs=whole,

time: 81.2 us -> 69.8 us (0.86)
  Pallas kernels: 21.6 us -> 12.3 us
  local copies, waits for them, and re-layouts: 8 us -> 6.05 us
    pallas_call x5, Pallas kernels: 13.8 us -> 4.55 us  [the longest x1 3.54 us: body(): pl.pallas_call(project_kernel, compiler_params=SOME_ROOM, out_shape=(chun...]
    ppermute x1, waiting for transfers between devices: 4.62 us -> 1.95 us  [body(): last_a = lax.ppermute(second_sum(from_b, 2), 'ch', pairing_a)]
    ppermute x1, waiting for transfers between devices: 0.42 us -> 2.88 us  [body(): last_b = lax.ppermute(second_sum(from_a, 0), 'ch', pairing_b)]
    unnamed x16 -> x6, local copies, waits for them, and re-layouts: 4.23 us -> 2.29 us
  transfers between devices with their start and end apart: 8 -> 8, of which waited for: 5 -> 5; matrix products, arithmetic and copies ran while one was open for 2% -> 2% of each run, Pallas kernels for 14% -> 5%
where the time goes in v3:
time: 69.8 us; the launch traced here: 69.3 us
  waiting for transfers between devices  28.4 us (41%)
  starting transfers between devices  21.1 us (30%)
  Pallas kernels  12.3 us (18%)
  local copies, waits for them, and re-layouts  6.05 us (9%)
  other arithmetic  1.26 us (2%)
    all_to_all x1, waiting for transfers between devices, body(): lax.all_to_all(jnp.broadcast_to(state[None], (blocks, modes, width)), 'ct...  14.8 us
    all_to_all x1, starting transfers between devices, body(): lax.all_to_all(jnp.broadcast_to(state[None], (blocks, modes, width)), 'ct...  9.94 us
    pallas_call x1, Pallas kernels, body(): pl.pallas_call(gate_project_kernel, out_shape=(jax.ShapeDtypeStruct((rows...  5.42 us
    ppermute x1, waiting for transfers between devices, body(): from_a = lax.ppermute(to_a, 'ch', pairing_a)  4.54 us
    ppermute x1, waiting for transfers between devices, body(): halo = lax.ppermute(edge, 'ctx', [(i, i + 1) for i in range(blocks - 1)])  4.25 us
    pallas_call x1, Pallas kernels, body(): pl.pallas_call(project_kernel, compiler_params=SOME_ROOM, out_shape=(chun...  3.54 us
    ppermute x1, starting transfers between devices, body(): halo = lax.ppermute(edge, 'ctx', [(i, i + 1) for i in range(blocks - 1)])  3.4 us
    ppermute x1, starting transfers between devices, body(): last_b = lax.ppermute(second_sum(from_a, 0), 'ch', pairing_b)  3.1 us
  transfers between devices with their start and end apart: 8, of which 5 were waited for; matrix products, arithmetic and copies ran while one was open for 2% of the time, Pallas kernels for 5%

profile of v3, /device:TPU:32, one launch (start us, length us, event | category | flops | bytes accessed | tf_op | source)
XLA Modules:
  0.0 69.3 jit_solution(4470273099795021335)
XLA Ops:
  0.0 0.7 %slice.12 = bf16[2,512]{1,0:T(2,128)(2,1)S(1)} slice(bf16[128,512]{1,0:T(8,128)(2,1)} %refs_0_.1), slice={[126:128], [0:512]} | slice | bytes 4096 | tf_op jit(solution)/shard_map/slice | solution.py:180
  0.7 0.7 %slice.10 = bf16[2,512]{1,0:T(2,128)(2,1)S(1)} slice(bf16[128,512]{1,0:T(8,128)(2,1)} %refs_1_.1), slice={[126:128], [0:512]} | slice | bytes 4096 | tf_op jit(solution)/shard_map/slice | solution.py:180
  1.4 0.7 %slice.11 = bf16[2,512]{1,0:T(2,128)(2,1)S(1)} slice(bf16[128,512]{1,0:T(8,128)(2,1)} %refs_2_.1), slice={[126:128], [0:512]} | slice | bytes 4096 | tf_op jit(solution)/shard_map/slice | solution.py:180
  2.1 3.4 %collective-permute-start = (bf16[8,512]{1,0:T(8,128)(2,1)S(1)}, bf16[8,512]{1,0:T(8,128)(2,1)S(1)}, u32[]{:S(2)}, u32[]{:S(2)}) collective-permute-start(bf16[8,512]{1,0:T(8,128)(2,1)S(1)} %pad_maximum_fusion), channel_id=1, source_target_pairs={{0,8},{8,16},{16,24},{24,32},{32,40},{40,48},{48,56},{56,64},{64,7... | collective-permute-start | bytes 24584 | tf_op jit(solution)/shard_map/ppermute | solution.py:182
  5.5 4.2 %collective-permute-done.halo_ref.refs_3_ = bf16[8,512]{1,0:T(8,128)(2,1)S(1)} collective-permute-done((bf16[8,512]{1,0:T(8,128)(2,1)S(1)}, bf16[8,512]{1,0:T(8,128)(2,1)S(1)}, u32[]{:S(2)}, u32[]{:S(2)}) %collective-permute-start) | collective-permute-done | bytes 8224 | tf_op jit(solution)/shard_map/ppermute | solution.py:182
  9.8 0.0 copy-start.2
  9.8 0.6 copy-done.2
  10.4 2.4 %shard_map.100 = (bf16[16,512]{1,0:T(8,128)(2,1)}, f32[16,8,512]{2,1,0:T(8,128)}) custom-call(bf16[128,512]{1,0:T(8,128)(2,1)} %refs_1_.1, bf16[128,512]{1,0:T(8,128)(2,1)} %refs_2_.1, bf16[8,512]{1,0:T(8,128)(2,1)} %copy-done.2, f32[3,3,512]{2,1,0:T(4,128)} %refs_4_.1, f32[16,512]{1,0:T(8,128)} %refs_6_.1), custom_call_target="tpu_custom_call" | custom-call | tf_op jit(solution)/shard_map/pallas_call | solution.py:185
  12.7 1.6 %broadcast_in_dim.14 = bf16[32,16,512]{2,1,0:T(8,128)(2,1)} broadcast(bf16[16,512]{1,0:T(8,128)(2,1)} %get-tuple-element.14), dimensions={1,2} | broadcast | bytes 540672 | tf_op jit(solution)/shard_map/broadcast_in_dim | solution.py:197
  14.3 9.9 %all-to-all-start = ((bf16[32,16,512]{2,1,0:T(8,128)(2,1)}), bf16[32,16,512]{2,1,0:T(8,128)(2,1)S(1)}, u32[]{:S(2)}, u32[]{:S(2)}) async-start(bf16[32,16,512]{2,1,0:T(8,128)(2,1)} %broadcast_in_dim.14), calls=%async_computation | async-start | bytes 1048576 | tf_op jit(solution)/shard_map/all_to_all | solution.py:196
  24.3 0.1 stack.14
  24.4 1.2 %multiply_add_fusion = (s32[8]{0:T(128)}, s32[8]{0:T(128)S(1)}) fusion(s32[8]{0:T(128)} %constant.39.clone, s32[8]{0:T(128)S(1)} %stack.14, s32[]{:T(128)S(6)} %sub.13, s32[]{:T(128)S(6)} %select_n.12), kind=kLoop, calls=%fused_computation.1 | loop fusion | flops 56 | bytes 136 | tf_op jit(solution)/shard_map/add | solution.py:210
  25.6 14.8 %all-to-all-done.refs_8_ = bf16[32,16,512]{2,1,0:T(8,128)(2,1)S(1)} async-done(((bf16[32,16,512]{2,1,0:T(8,128)(2,1)}), bf16[32,16,512]{2,1,0:T(8,128)(2,1)S(1)}, u32[]{:S(2)}, u32[]{:S(2)}) %all-to-all-start) | async-done | bytes 524320 | tf_op jit(solution)/shard_map/all_to_all | solution.py:196
  40.4 0.0 copy-start.1
  40.4 0.8 %copy-done.1 = bf16[32,16,512]{2,1,0:T(8,128)(2,1)} copy-done((bf16[32,16,512]{2,1,0:T(8,128)(2,1)}, bf16[32,16,512]{2,1,0:T(8,128)(2,1)S(1)}, u32[]{:S(2)}) %copy-start.1) | copy-done | bytes 524312
  41.2 5.4 %shard_map.101 = (bf16[128,512]{1,0:T(8,128)(2,1)}, bf16[4,128,512]{2,1,0:T(8,128)(2,1)}, bf16[4,128,512]{2,1,0:T(8,128)(2,1)}) custom-call(s32[1]{0:T(128)} %bitcast.4.ctx_ref, s32[8]{0:T(128)} %get-tuple-element.23.order_ref, bf16[128,512]{1,0:T(8,128)(2,1)} %refs_0_.1, bf16[128,512]{1,0:T(8,128)(2,1)} %refs_1_.1, bf16[128,512]{1,0:T(8,128)(2,1)} %refs_2_.1, ...), custom_call_target="tpu_custom_call" | custom-call | tf_op jit(solution)/shard_map/pallas_call | solution.py:219
  46.6 0.1 collective-permute-start.2
  46.7 0.5 collective-permute-start.1
  47.2 0.0 copy-start
  47.2 0.9 %copy-done = bf16[128,512]{1,0:T(8,128)(2,1)S(1)} copy-done((bf16[128,512]{1,0:T(8,128)(2,1)S(1)}, bf16[128,512]{1,0:T(8,128)(2,1)}, u32[]{:S(2)}) %copy-start) | copy-done | bytes 131096
  48.1 3.5 %shard_map.102 = (f32[4,128,512]{2,1,0:T(8,128)S(1)}, f32[4,128,512]{2,1,0:T(8,128)S(1)}) custom-call(s32[8]{0:T(128)S(1)} %get-tuple-element.24.order_ref, bf16[128,512]{1,0:T(8,128)(2,1)S(1)} %copy-done, bf16[512,8192]{1,0:T(8,128)(2,1)} %weight_ref.1), custom_call_target="tpu_custom_call" | custom-call | flops 536870912 | bytes 4194304 | tf_op jit(solution)/shard_map/pallas_call | solution.py:235
  51.7 0.0 collective-permute-done.2.swapped_ref
  51.7 0.1 shard_map.103
  51.8 1.7 %collective-permute-start.3 = (bf16[2,128,512]{2,1,0:T(8,128)(2,1)S(1)}, bf16[2,128,512]{2,1,0:T(8,128)(2,1)S(1)}, u32[]{:S(2)}, u32[]{:S(2)}) collective-permute-start(bf16[2,128,512]{2,1,0:T(8,128)(2,1)S(1)} %get-tuple-element.21), channel_id=1, source_target_pairs={{0,2},{1,3},{2,0},{3,1},{4,6},{5,7},{6,4},{7,5},{8,10},{9,11},{10,... | collective-permute-start | bytes 786440 | tf_op jit(solution)/shard_map/ppermute | solution.py:250
  53.4 2.2 %collective-permute-start.4 = (bf16[2,128,512]{2,1,0:T(8,128)(2,1)S(1)}, bf16[2,128,512]{2,1,0:T(8,128)(2,1)S(1)}, u32[]{:S(2)}, u32[]{:S(2)}) collective-permute-start(bf16[2,128,512]{2,1,0:T(8,128)(2,1)S(1)} %get-tuple-element.22), channel_id=1, source_target_pairs={{0,6},{1,7},{2,4},{3,5},{4,2},{5,3},{6,0},{7,1},{8,14},{9,15},{10,... | collective-permute-start | bytes 786440 | tf_op jit(solution)/shard_map/ppermute | solution.py:251
  55.6 0.0 collective-permute-done.1.swapped_ref
  55.6 4.5 %collective-permute-done.3.from_ref.from_a_ref = bf16[2,128,512]{2,1,0:T(8,128)(2,1)S(1)} collective-permute-done((bf16[2,128,512]{2,1,0:T(8,128)(2,1)S(1)}, bf16[2,128,512]{2,1,0:T(8,128)(2,1)S(1)}, u32[]{:S(2)}, u32[]{:S(2)}) %collective-permute-start.3) | collective-permute-done | bytes 262176 | tf_op jit(solution)/shard_map/ppermute | solution.py:250
  60.2 3.1 %collective-permute-start.5 = (bf16[128,512]{1,0:T(8,128)(2,1)S(1)}, bf16[128,512]{1,0:T(8,128)(2,1)S(1)}, u32[]{:S(2)}, u32[]{:S(2)}) collective-permute-start(bf16[128,512]{1,0:T(8,128)(2,1)S(1)} %shard_map.104), channel_id=1, source_target_pairs={{0,6},{1,7},{2,4},{3,5},{4,2},{5,3},{6,0},{7,1},{8,14},{9,15},{10,... | collective-permute-start | bytes 393224 | tf_op jit(solution)/shard_map/ppermute | solution.py:262
  63.3 0.0 collective-permute-done.4.from_ref.from_b_ref
  63.4 0.2 collective-permute-start.6
  63.6 2.9 %collective-permute-done.5.last_b_ref = bf16[128,512]{1,0:T(8,128)(2,1)S(1)} collective-permute-done((bf16[128,512]{1,0:T(8,128)(2,1)S(1)}, bf16[128,512]{1,0:T(8,128)(2,1)S(1)}, u32[]{:S(2)}, u32[]{:S(2)}) %collective-permute-start.5) | collective-permute-done | bytes 131104 | tf_op jit(solution)/shard_map/ppermute | solution.py:262
  66.5 1.9 %collective-permute-done.6.last_a_ref = bf16[128,512]{1,0:T(8,128)(2,1)S(1)} collective-permute-done((bf16[128,512]{1,0:T(8,128)(2,1)S(1)}, bf16[128,512]{1,0:T(8,128)(2,1)S(1)}, u32[]{:S(2)}, u32[]{:S(2)}) %collective-permute-start.6) | collective-permute-done | bytes 131104 | tf_op jit(solution)/shard_map/ppermute | solution.py:263
  68.4 0.8 %shard_map.106 = bf16[128,1024]{1,0:T(8,128)(2,1)} custom-call(f32[4,128,512]{2,1,0:T(8,128)S(1)} %get-tuple-element.17.kept_ref, bf16[4,128,512]{2,1,0:T(8,128)(2,1)S(1)} %collective-permute-done.1.swapped_ref, bf16[2,128,512]{2,1,0:T(8,128)(2,1)S(1)} %collective-permute-done.3.from_ref.from_a_ref, ...), custom_call_target="tpu_custom_call" | custom-call | tf_op jit(solution)/shard_map/pallas_call | solution.py:264
  (3 shorter events, 0.1 us)
Async XLA Ops:
  2.1 7.7 %collective-permute-start = (bf16[8,512]{1,0:T(8,128)(2,1)S(1)}, bf16[8,512]{1,0:T(8,128)(2,1)S(1)}, u32[]{:S(2)}, u32[]{:S(2)}) collective-permute-start(bf16[8,512]{1,0:T(8,128)(2,1)S(1)} %pad_maximum_fusion), channel_id=1, source_target_pairs={{0,8},{8,16},{16,24},{24,32},{32,40},{40,48},{48,56},{56,64},{64,7... | collective-permute-start | bytes 24584 | tf_op jit(solution)/shard_map/ppermute | solution.py:182
  9.8 0.6 copy-start.2
  14.3 26.1 %all-to-all-start = ((bf16[32,16,512]{2,1,0:T(8,128)(2,1)}), bf16[32,16,512]{2,1,0:T(8,128)(2,1)S(1)}, u32[]{:S(2)}, u32[]{:S(2)}) async-start(bf16[32,16,512]{2,1,0:T(8,128)(2,1)} %broadcast_in_dim.14), calls=%async_computation | async-start | bytes 1048576 | tf_op jit(solution)/shard_map/all_to_all | solution.py:196
  40.4 0.8 %copy-start.1 = (bf16[32,16,512]{2,1,0:T(8,128)(2,1)}, bf16[32,16,512]{2,1,0:T(8,128)(2,1)S(1)}, u32[]{:S(2)}) copy-start(bf16[32,16,512]{2,1,0:T(8,128)(2,1)S(1)} %all-to-all-done.refs_8_) | copy-start | bytes 1572868
  46.6 5.1 %collective-permute-start.2 = (bf16[4,128,512]{2,1,0:T(8,128)(2,1)}, bf16[4,128,512]{2,1,0:T(8,128)(2,1)S(1)}, u32[]{:S(2)}, u32[]{:S(2)}) collective-permute-start(bf16[4,128,512]{2,1,0:T(8,128)(2,1)} %get-tuple-element.20), channel_id=1, source_target_pairs={{0,1},{1,0},{2,3},{3,2},{4,5},{5,4},{6,7},{7,6},{8,9},{9,8},{10,11... | collective-permute-start | bytes 1572872 | tf_op jit(solution)/shard_map/ppermute | solution.py:233
  46.7 8.9 %collective-permute-start.1 = (bf16[4,128,512]{2,1,0:T(8,128)(2,1)}, bf16[4,128,512]{2,1,0:T(8,128)(2,1)S(1)}, u32[]{:S(2)}, u32[]{:S(2)}) collective-permute-start(bf16[4,128,512]{2,1,0:T(8,128)(2,1)} %get-tuple-element.18), channel_id=1, source_target_pairs={{0,1},{1,0},{2,3},{3,2},{4,5},{5,4},{6,7},{7,6},{8,9},{9,8},{10,11... | collective-permute-start | bytes 1572872 | tf_op jit(solution)/shard_map/ppermute | solution.py:234
  47.2 0.9 %copy-start = (bf16[128,512]{1,0:T(8,128)(2,1)S(1)}, bf16[128,512]{1,0:T(8,128)(2,1)}, u32[]{:S(2)}) copy-start(bf16[128,512]{1,0:T(8,128)(2,1)} %get-tuple-element.16.gated_ref) | copy-start | bytes 393220
  51.8 8.4 %collective-permute-start.3 = (bf16[2,128,512]{2,1,0:T(8,128)(2,1)S(1)}, bf16[2,128,512]{2,1,0:T(8,128)(2,1)S(1)}, u32[]{:S(2)}, u32[]{:S(2)}) collective-permute-start(bf16[2,128,512]{2,1,0:T(8,128)(2,1)S(1)} %get-tuple-element.21), channel_id=1, source_target_pairs={{0,2},{1,3},{2,0},{3,1},{4,6},{5,7},{6,4},{7,5},{8,10},{9,11},{10,... | collective-permute-start | bytes 786440 | tf_op jit(solution)/shard_map/ppermute | solution.py:250
  53.4 9.9 %collective-permute-start.4 = (bf16[2,128,512]{2,1,0:T(8,128)(2,1)S(1)}, bf16[2,128,512]{2,1,0:T(8,128)(2,1)S(1)}, u32[]{:S(2)}, u32[]{:S(2)}) collective-permute-start(bf16[2,128,512]{2,1,0:T(8,128)(2,1)S(1)} %get-tuple-element.22), channel_id=1, source_target_pairs={{0,6},{1,7},{2,4},{3,5},{4,2},{5,3},{6,0},{7,1},{8,14},{9,15},{10,... | collective-permute-start | bytes 786440 | tf_op jit(solution)/shard_map/ppermute | solution.py:251
  60.2 6.3 %collective-permute-start.5 = (bf16[128,512]{1,0:T(8,128)(2,1)S(1)}, bf16[128,512]{1,0:T(8,128)(2,1)S(1)}, u32[]{:S(2)}, u32[]{:S(2)}) collective-permute-start(bf16[128,512]{1,0:T(8,128)(2,1)S(1)} %shard_map.104), channel_id=1, source_target_pairs={{0,6},{1,7},{2,4},{3,5},{4,2},{5,3},{6,0},{7,1},{8,14},{9,15},{10,... | collective-permute-start | bytes 393224 | tf_op jit(solution)/shard_map/ppermute | solution.py:262
  63.4 5.1 %collective-permute-start.6 = (bf16[128,512]{1,0:T(8,128)(2,1)S(1)}, bf16[128,512]{1,0:T(8,128)(2,1)S(1)}, u32[]{:S(2)}, u32[]{:S(2)}) collective-permute-start(bf16[128,512]{1,0:T(8,128)(2,1)S(1)} %shard_map.105), channel_id=1, source_target_pairs={{0,2},{1,3},{2,0},{3,1},{4,6},{5,7},{6,4},{7,5},{8,10},{9,11},{10,... | collective-permute-start | bytes 393224 | tf_op jit(solution)/shard_map/ppermute | solution.py:263

commit v4 on v3

--- a/solution.py
+++ b/solution.py
@@ -33,6 +33,20 @@
 
 def spread(row):
     return jnp.broadcast_to(row, (SUBLANES, row.shape[-1]))
+
+
+def edge_kernel(k_ref, v_ref, q_ref, edge_ref, tails, arrived):
+    rows, height = k_ref.shape[0], tails.shape[1]
+    copies = [
+        pltpu.make_async_copy(ref.at[pl.ds(rows - height, height), :], tails.at[i], arrived.at[i])
+        for i, ref in enumerate((k_ref, v_ref, q_ref))
+    ]
+    for copy in copies:
+        copy.start()
+    for copy in copies:
+        copy.wait()
+    pieces = [tails[i].astype(F32)[height - 2 :] for i in (0, 1, 2, 2)]
+    edge_ref[...] = jnp.concatenate(pieces, axis=0).astype(edge_ref.dtype)
 
 
 def state_kernel(k_ref, v_ref, halo_ref, taps_ref, rate_ref, state_ref, ends_ref, mixed):
@@ -58,7 +72,9 @@
             ends_ref[r, :, cols] = held[r]
             weight = jnp.exp(-spread(rate[r : r + 1]) * left)
             totals.append(jnp.sum(weight * held[r], axis=0, keepdims=True))
-        state_ref[:, cols] = jnp.concatenate(totals, axis=0).astype(state_ref.dtype)
+        total = jnp.concatenate(totals, axis=0).astype(state_ref.dtype)
+        for j in range(state_ref.shape[0]):
+            state_ref[j, :, cols] = total
 
 
 def gate_kernel(
@@ -175,17 +191,20 @@
     chips = parts // 2
     rows, width = query_input.shape
     modes = residue.shape[0]
-    last = rows - (short_weight.shape[1] - 1)
-    edge = jnp.concatenate(
-        [key_input[last:], value_input[last:], query_input[last:], query_input[last:]], axis=0
-    )
+    whole = pl.BlockSpec(memory_space=pltpu.VMEM)
+    edge = pl.pallas_call(
+        edge_kernel,
+        out_shape=jax.ShapeDtypeStruct((SUBLANES, width), BF16),
+        in_specs=[pl.BlockSpec(memory_space=pl.ANY)] * 3,
+        out_specs=whole,
+        scratch_shapes=[pltpu.VMEM((3, 16, width), BF16), pltpu.SemaphoreType.DMA((3,))],
+    )(key_input, value_input, query_input)
     halo = lax.ppermute(edge, "ctx", [(i, i + 1) for i in range(blocks - 1)])
 
-    whole = pl.BlockSpec(memory_space=pltpu.VMEM)
-    state, ends = pl.pallas_call(
+    state_copies, ends = pl.pallas_call(
         state_kernel,
         out_shape=(
-            jax.ShapeDtypeStruct((modes, width), BF16),
+            jax.ShapeDtypeStruct((blocks, modes, width), BF16),
             jax.ShapeDtypeStruct((modes, SUBLANES, width), F32),
         ),
         in_specs=[whole] * 5,
@@ -193,9 +212,7 @@
         scratch_shapes=[pltpu.VMEM((width // LANES, rows, LANES), F32)],
     )(key_input, value_input, halo, short_weight, decay_rate)
 
-    states = lax.all_to_all(
-        jnp.broadcast_to(state[None], (blocks, modes, width)), "ctx", 0, 0
-    )
+    states = lax.all_to_all(state_copies, "ctx", 0, 0)
 
     partner_core = [(i, i ^ 1) for i in range(parts)]
     pairing_a = [(i, (i // 2 ^ 1) * 2 + i % 2) for i in range(parts)]

time: 69.8 us -> 67.8 us (0.971)
  local copies, waits for them, and re-layouts: 6.05 us -> 2.38 us
  Pallas kernels: 12.3 us -> 14 us
    slice x3 -> x0, local copies, waits for them, and re-layouts: 2.1 us -> none  [the longest x1 0.7 us: body(): query_input[last:]]
    pallas_call x1 -> x2, Pallas kernels: 2.37 us -> 3.99 us  [the longest x1 2.61 us: body(): pl.pallas_call(state_kernel, out_shape=(jax.ShapeDtypeStruct((blocks, mod...]
    broadcast_in_dim x1 -> x0, local copies, waits for them, and re-layouts: 1.57 us -> none  [body(): jnp.broadcast_to(state[None], (blocks, modes, width))]
  transfers between devices with their start and end apart: 8 -> 8, of which waited for: 5 -> 5; matrix products, arithmetic and copies ran while one was open for 2% -> 2% of each run, Pallas kernels for 5% -> 6%
where the time goes in v4:
time: 67.8 us; the launch traced here: 67.4 us
  waiting for transfers between devices  28.6 us (42%)
  starting transfers between devices  21.1 us (31%)
  Pallas kernels  14 us (21%)
  local copies, waits for them, and re-layouts  2.38 us (4%)
  other arithmetic  1.24 us (2%)
    all_to_all x1, waiting for transfers between devices, body(): states = lax.all_to_all(state_copies, 'ctx', 0, 0)  14.8 us
    all_to_all x1, starting transfers between devices, body(): states = lax.all_to_all(state_copies, 'ctx', 0, 0)  9.94 us
    pallas_call x1, Pallas kernels, body(): pl.pallas_call(gate_project_kernel, out_shape=(jax.ShapeDtypeStruct((rows...  5.43 us
    ppermute x1, waiting for transfers between devices, body(): from_a = lax.ppermute(to_a, 'ch', pairing_a)  4.54 us
    ppermute x1, waiting for transfers between devices, body(): halo = lax.ppermute(edge, 'ctx', [(i, i + 1) for i in range(blocks - 1)])  4.46 us
    pallas_call x1, Pallas kernels, body(): pl.pallas_call(project_kernel, compiler_params=SOME_ROOM, out_shape=(chun...  3.54 us
    ppermute x1, starting transfers between devices, body(): halo = lax.ppermute(edge, 'ctx', [(i, i + 1) for i in range(blocks - 1)])  3.4 us
    ppermute x1, starting transfers between devices, body(): last_b = lax.ppermute(second_sum(from_a, 0), 'ch', pairing_b)  3.1 us
  transfers between devices with their start and end apart: 8, of which 5 were waited for; matrix products, arithmetic and copies ran while one was open for 2% of the time, Pallas kernels for 6%

profile of v4, /device:TPU:32, one launch (start us, length us, event | category | flops | bytes accessed | tf_op | source)
XLA Modules:
  0.0 67.4 jit_solution(10315039850775669543)
XLA Ops:
  0.0 1.4 %shard_map.100 = bf16[8,512]{1,0:T(8,128)(2,1)} custom-call(bf16[128,512]{1,0:T(8,128)(2,1)} %refs_1_.1, bf16[128,512]{1,0:T(8,128)(2,1)} %refs_2_.1, bf16[128,512]{1,0:T(8,128)(2,1)} %refs_0_.1), custom_call_target="tpu_custom_call" | custom-call | tf_op jit(solution)/shard_map/pallas_call | solution.py:195
  1.4 3.4 %collective-permute-start = (bf16[8,512]{1,0:T(8,128)(2,1)}, bf16[8,512]{1,0:T(8,128)(2,1)S(1)}, u32[]{:S(2)}, u32[]{:S(2)}) collective-permute-start(bf16[8,512]{1,0:T(8,128)(2,1)} %shard_map.100), channel_id=1, source_target_pairs={{0,8},{8,16},{16,24},{24,32},{32,40},{40,48},{48,56},{56,64},{64,7... | collective-permute-start | bytes 24584 | tf_op jit(solution)/shard_map/ppermute | solution.py:202
  4.8 4.5 %collective-permute-done.halo_ref.refs_3_ = bf16[8,512]{1,0:T(8,128)(2,1)S(1)} collective-permute-done((bf16[8,512]{1,0:T(8,128)(2,1)}, bf16[8,512]{1,0:T(8,128)(2,1)S(1)}, u32[]{:S(2)}, u32[]{:S(2)}) %collective-permute-start) | collective-permute-done | bytes 8224 | tf_op jit(solution)/shard_map/ppermute | solution.py:202
  9.3 0.0 copy-start.2
  9.3 0.6 copy-done.2
  9.8 2.6 %shard_map.101 = (bf16[32,16,512]{2,1,0:T(8,128)(2,1)}, f32[16,8,512]{2,1,0:T(8,128)}) custom-call(bf16[128,512]{1,0:T(8,128)(2,1)} %refs_1_.1, bf16[128,512]{1,0:T(8,128)(2,1)} %refs_2_.1, bf16[8,512]{1,0:T(8,128)(2,1)} %copy-done.2, f32[3,3,512]{2,1,0:T(4,128)} %refs_4_.1, f32[16,512]{1,0:T(8,128)} %refs_6_.1), custom_call_target="tpu_custom_call" | custom-call | tf_op jit(solution)/shard_map/pallas_call | solution.py:204
  12.5 9.9 %all-to-all-start = ((bf16[32,16,512]{2,1,0:T(8,128)(2,1)}), bf16[32,16,512]{2,1,0:T(8,128)(2,1)S(1)}, u32[]{:S(2)}, u32[]{:S(2)}) async-start(bf16[32,16,512]{2,1,0:T(8,128)(2,1)} %get-tuple-element.14), calls=%async_computation | async-start | bytes 1048576 | tf_op jit(solution)/shard_map/all_to_all | solution.py:215
  22.4 0.1 stack.14
  22.5 1.2 %multiply_add_fusion = (s32[8]{0:T(128)}, s32[8]{0:T(128)S(1)}) fusion(s32[8]{0:T(128)} %constant.39.clone, s32[8]{0:T(128)S(1)} %stack.14, s32[]{:T(128)S(6)} %sub.13, s32[]{:T(128)S(6)} %select_n.12), kind=kLoop, calls=%fused_computation | loop fusion | flops 56 | bytes 136 | tf_op jit(solution)/shard_map/add | solution.py:227
  23.8 14.8 %all-to-all-done.refs_8_ = bf16[32,16,512]{2,1,0:T(8,128)(2,1)S(1)} async-done(((bf16[32,16,512]{2,1,0:T(8,128)(2,1)}), bf16[32,16,512]{2,1,0:T(8,128)(2,1)S(1)}, u32[]{:S(2)}, u32[]{:S(2)}) %all-to-all-start) | async-done | bytes 524320 | tf_op jit(solution)/shard_map/all_to_all | solution.py:215
  38.5 0.0 copy-start.1
  38.5 0.8 %copy-done.1 = bf16[32,16,512]{2,1,0:T(8,128)(2,1)} copy-done((bf16[32,16,512]{2,1,0:T(8,128)(2,1)}, bf16[32,16,512]{2,1,0:T(8,128)(2,1)S(1)}, u32[]{:S(2)}) %copy-start.1) | copy-done | bytes 524312
  39.3 5.4 %shard_map.102 = (bf16[128,512]{1,0:T(8,128)(2,1)}, bf16[4,128,512]{2,1,0:T(8,128)(2,1)}, bf16[4,128,512]{2,1,0:T(8,128)(2,1)}) custom-call(s32[1]{0:T(128)} %bitcast.4.ctx_ref, s32[8]{0:T(128)} %get-tuple-element.23.order_ref, bf16[128,512]{1,0:T(8,128)(2,1)} %refs_0_.1, bf16[128,512]{1,0:T(8,128)(2,1)} %refs_1_.1, bf16[128,512]{1,0:T(8,128)(2,1)} %refs_2_.1, ...), custom_call_target="tpu_custom_call" | custom-call | tf_op jit(solution)/shard_map/pallas_call | solution.py:236
  44.8 0.1 collective-permute-start.2
  44.9 0.5 collective-permute-start.1
  45.4 0.0 copy-start
  45.4 0.9 %copy-done = bf16[128,512]{1,0:T(8,128)(2,1)S(1)} copy-done((bf16[128,512]{1,0:T(8,128)(2,1)S(1)}, bf16[128,512]{1,0:T(8,128)(2,1)}, u32[]{:S(2)}) %copy-start) | copy-done | bytes 131096
  46.3 3.5 %shard_map.103 = (f32[4,128,512]{2,1,0:T(8,128)S(1)}, f32[4,128,512]{2,1,0:T(8,128)S(1)}) custom-call(s32[8]{0:T(128)S(1)} %get-tuple-element.24.order_ref, bf16[128,512]{1,0:T(8,128)(2,1)S(1)} %copy-done, bf16[512,8192]{1,0:T(8,128)(2,1)} %weight_ref.1), custom_call_target="tpu_custom_call" | custom-call | flops 536870912 | bytes 4194304 | tf_op jit(solution)/shard_map/pallas_call | solution.py:252
  49.8 0.0 collective-permute-done.2.swapped_ref
  49.8 0.1 shard_map.104
  49.9 1.7 %collective-permute-start.3 = (bf16[2,128,512]{2,1,0:T(8,128)(2,1)S(1)}, bf16[2,128,512]{2,1,0:T(8,128)(2,1)S(1)}, u32[]{:S(2)}, u32[]{:S(2)}) collective-permute-start(bf16[2,128,512]{2,1,0:T(8,128)(2,1)S(1)} %get-tuple-element.21), channel_id=1, source_target_pairs={{0,2},{1,3},{2,0},{3,1},{4,6},{5,7},{6,4},{7,5},{8,10},{9,11},{10,... | collective-permute-start | bytes 786440 | tf_op jit(solution)/shard_map/ppermute | solution.py:267
  51.6 2.2 %collective-permute-start.4 = (bf16[2,128,512]{2,1,0:T(8,128)(2,1)S(1)}, bf16[2,128,512]{2,1,0:T(8,128)(2,1)S(1)}, u32[]{:S(2)}, u32[]{:S(2)}) collective-permute-start(bf16[2,128,512]{2,1,0:T(8,128)(2,1)S(1)} %get-tuple-element.22), channel_id=1, source_target_pairs={{0,6},{1,7},{2,4},{3,5},{4,2},{5,3},{6,0},{7,1},{8,14},{9,15},{10,... | collective-permute-start | bytes 786440 | tf_op jit(solution)/shard_map/ppermute | solution.py:268
  53.8 0.0 collective-permute-done.1.swapped_ref
  53.8 4.5 %collective-permute-done.3.from_ref.from_a_ref = bf16[2,128,512]{2,1,0:T(8,128)(2,1)S(1)} collective-permute-done((bf16[2,128,512]{2,1,0:T(8,128)(2,1)S(1)}, bf16[2,128,512]{2,1,0:T(8,128)(2,1)S(1)}, u32[]{:S(2)}, u32[]{:S(2)}) %collective-permute-start.3) | collective-permute-done | bytes 262176 | tf_op jit(solution)/shard_map/ppermute | solution.py:267
  58.4 3.1 %collective-permute-start.5 = (bf16[128,512]{1,0:T(8,128)(2,1)S(1)}, bf16[128,512]{1,0:T(8,128)(2,1)S(1)}, u32[]{:S(2)}, u32[]{:S(2)}) collective-permute-start(bf16[128,512]{1,0:T(8,128)(2,1)S(1)} %shard_map.105), channel_id=1, source_target_pairs={{0,6},{1,7},{2,4},{3,5},{4,2},{5,3},{6,0},{7,1},{8,14},{9,15},{10,... | collective-permute-start | bytes 393224 | tf_op jit(solution)/shard_map/ppermute | solution.py:279
  61.5 0.0 collective-permute-done.4.from_ref.from_b_ref
  61.5 0.2 collective-permute-start.6
  61.7 2.9 %collective-permute-done.5.last_b_ref = bf16[128,512]{1,0:T(8,128)(2,1)S(1)} collective-permute-done((bf16[128,512]{1,0:T(8,128)(2,1)S(1)}, bf16[128,512]{1,0:T(8,128)(2,1)S(1)}, u32[]{:S(2)}, u32[]{:S(2)}) %collective-permute-start.5) | collective-permute-done | bytes 131104 | tf_op jit(solution)/shard_map/ppermute | solution.py:279
  64.6 1.9 %collective-permute-done.6.last_a_ref = bf16[128,512]{1,0:T(8,128)(2,1)S(1)} collective-permute-done((bf16[128,512]{1,0:T(8,128)(2,1)S(1)}, bf16[128,512]{1,0:T(8,128)(2,1)S(1)}, u32[]{:S(2)}, u32[]{:S(2)}) %collective-permute-start.6) | collective-permute-done | bytes 131104 | tf_op jit(solution)/shard_map/ppermute | solution.py:280
  66.6 0.8 %shard_map.107 = bf16[128,1024]{1,0:T(8,128)(2,1)} custom-call(f32[4,128,512]{2,1,0:T(8,128)S(1)} %get-tuple-element.17.kept_ref, bf16[4,128,512]{2,1,0:T(8,128)(2,1)S(1)} %collective-permute-done.1.swapped_ref, bf16[2,128,512]{2,1,0:T(8,128)(2,1)S(1)} %collective-permute-done.3.from_ref.from_a_ref, ...), custom_call_target="tpu_custom_call" | custom-call | tf_op jit(solution)/shard_map/pallas_call | solution.py:281
  (2 shorter events, 0.1 us)
Async XLA Ops:
  1.4 7.9 %collective-permute-start = (bf16[8,512]{1,0:T(8,128)(2,1)}, bf16[8,512]{1,0:T(8,128)(2,1)S(1)}, u32[]{:S(2)}, u32[]{:S(2)}) collective-permute-start(bf16[8,512]{1,0:T(8,128)(2,1)} %shard_map.100), channel_id=1, source_target_pairs={{0,8},{8,16},{16,24},{24,32},{32,40},{40,48},{48,56},{56,64},{64,7... | collective-permute-start | bytes 24584 | tf_op jit(solution)/shard_map/ppermute | solution.py:202
  9.3 0.6 copy-start.2
  12.5 26.1 %all-to-all-start = ((bf16[32,16,512]{2,1,0:T(8,128)(2,1)}), bf16[32,16,512]{2,1,0:T(8,128)(2,1)S(1)}, u32[]{:S(2)}, u32[]{:S(2)}) async-start(bf16[32,16,512]{2,1,0:T(8,128)(2,1)} %get-tuple-element.14), calls=%async_computation | async-start | bytes 1048576 | tf_op jit(solution)/shard_map/all_to_all | solution.py:215
  38.5 0.8 %copy-start.1 = (bf16[32,16,512]{2,1,0:T(8,128)(2,1)}, bf16[32,16,512]{2,1,0:T(8,128)(2,1)S(1)}, u32[]{:S(2)}) copy-start(bf16[32,16,512]{2,1,0:T(8,128)(2,1)S(1)} %all-to-all-done.refs_8_) | copy-start | bytes 1572868
  44.8 5.1 %collective-permute-start.2 = (bf16[4,128,512]{2,1,0:T(8,128)(2,1)}, bf16[4,128,512]{2,1,0:T(8,128)(2,1)S(1)}, u32[]{:S(2)}, u32[]{:S(2)}) collective-permute-start(bf16[4,128,512]{2,1,0:T(8,128)(2,1)} %get-tuple-element.20), channel_id=1, source_target_pairs={{0,1},{1,0},{2,3},{3,2},{4,5},{5,4},{6,7},{7,6},{8,9},{9,8},{10,11... | collective-permute-start | bytes 1572872 | tf_op jit(solution)/shard_map/ppermute | solution.py:250
  44.9 8.9 %collective-permute-start.1 = (bf16[4,128,512]{2,1,0:T(8,128)(2,1)}, bf16[4,128,512]{2,1,0:T(8,128)(2,1)S(1)}, u32[]{:S(2)}, u32[]{:S(2)}) collective-permute-start(bf16[4,128,512]{2,1,0:T(8,128)(2,1)} %get-tuple-element.18), channel_id=1, source_target_pairs={{0,1},{1,0},{2,3},{3,2},{4,5},{5,4},{6,7},{7,6},{8,9},{9,8},{10,11... | collective-permute-start | bytes 1572872 | tf_op jit(solution)/shard_map/ppermute | solution.py:251
  45.4 0.9 %copy-start = (bf16[128,512]{1,0:T(8,128)(2,1)S(1)}, bf16[128,512]{1,0:T(8,128)(2,1)}, u32[]{:S(2)}) copy-start(bf16[128,512]{1,0:T(8,128)(2,1)} %get-tuple-element.16.gated_ref) | copy-start | bytes 393220
  49.9 8.4 %collective-permute-start.3 = (bf16[2,128,512]{2,1,0:T(8,128)(2,1)S(1)}, bf16[2,128,512]{2,1,0:T(8,128)(2,1)S(1)}, u32[]{:S(2)}, u32[]{:S(2)}) collective-permute-start(bf16[2,128,512]{2,1,0:T(8,128)(2,1)S(1)} %get-tuple-element.21), channel_id=1, source_target_pairs={{0,2},{1,3},{2,0},{3,1},{4,6},{5,7},{6,4},{7,5},{8,10},{9,11},{10,... | collective-permute-start | bytes 786440 | tf_op jit(solution)/shard_map/ppermute | solution.py:267
  51.6 9.9 %collective-permute-start.4 = (bf16[2,128,512]{2,1,0:T(8,128)(2,1)S(1)}, bf16[2,128,512]{2,1,0:T(8,128)(2,1)S(1)}, u32[]{:S(2)}, u32[]{:S(2)}) collective-permute-start(bf16[2,128,512]{2,1,0:T(8,128)(2,1)S(1)} %get-tuple-element.22), channel_id=1, source_target_pairs={{0,6},{1,7},{2,4},{3,5},{4,2},{5,3},{6,0},{7,1},{8,14},{9,15},{10,... | collective-permute-start | bytes 786440 | tf_op jit(solution)/shard_map/ppermute | solution.py:268
  58.4 6.3 %collective-permute-start.5 = (bf16[128,512]{1,0:T(8,128)(2,1)S(1)}, bf16[128,512]{1,0:T(8,128)(2,1)S(1)}, u32[]{:S(2)}, u32[]{:S(2)}) collective-permute-start(bf16[128,512]{1,0:T(8,128)(2,1)S(1)} %shard_map.105), channel_id=1, source_target_pairs={{0,6},{1,7},{2,4},{3,5},{4,2},{5,3},{6,0},{7,1},{8,14},{9,15},{10,... | collective-permute-start | bytes 393224 | tf_op jit(solution)/shard_map/ppermute | solution.py:279
  61.5 5.1 %collective-permute-start.6 = (bf16[128,512]{1,0:T(8,128)(2,1)S(1)}, bf16[128,512]{1,0:T(8,128)(2,1)S(1)}, u32[]{:S(2)}, u32[]{:S(2)}) collective-permute-start(bf16[128,512]{1,0:T(8,128)(2,1)S(1)} %shard_map.106), channel_id=1, source_target_pairs={{0,2},{1,3},{2,0},{3,1},{4,6},{5,7},{6,4},{7,5},{8,10},{9,11},{10,... | collective-permute-start | bytes 393224 | tf_op jit(solution)/shard_map/ppermute | solution.py:280
